TPU v7x, 32 devices: a whole 2x2x4 slice. The times are simulated.
32 devices in a mesh: wide: 16 (over z, y, core), narrow: 2 (over x).
Axes of the slice: x: 2, y: 2, z: 4, core: 2. Of those that a mesh axis runs over, the one named last changes fastest.
Arguments:
- valence: float32 [8, 32768], P(None, ('wide', 'narrow')), may hold values from -6 to 6
- conduction: float32 [32, 32768], P(('wide', 'narrow')), may hold values from -6 to 6
- eps_val: float32 [8], replicated, may hold values from -12 to -2
- eps_cond: float32 [32], replicated, may hold values from 0.5 to 20
- omega: float32 [6], replicated, may hold values from 0.3 to 30
- gmap: int32 [8192], replicated, may hold values from 0 to 32767, as said below
Outputs:
- chi: float32 [6, 8192, 8192], P(None, 'wide', 'narrow')
Inputs may be any that keep to these rules, and one draw needn't show every extreme that they name: `gmap`: distinct grid indices: the 8192 grid points of smallest squared wave vector (frequencies folded to -16 .. 15), equal lengths in random order, listed by rising length.
All inputs are finite; a program needn't handle non-finite values.
Results may differ from a plain program's by a relative error of at most 0.0042.
Values may be sent and summed in bfloat16 or wider, within the bound.
A program may use at most 128 MiB of HBM per device.

v0:
```python
import functools
import math

import jax
import jax.numpy as jnp
import numpy as np
from jax import lax
from jax.experimental import pallas as pl
from jax.experimental.pallas import tpu as pltpu
from jax.sharding import PartitionSpec as P

GRID = 32
MESH = pl.DeviceIdType.MESH
VMEM = pltpu.MemorySpace.VMEM
HBM = pltpu.MemorySpace.HBM
SMEM = pltpu.MemorySpace.SMEM


def wide_factors(wide):
    chips = wide // 2
    inner = 2 ** (int(math.log2(chips)) // 2)
    return chips // inner, inner


def gather_kernel(wide, narrow, split, row_width, row_step, src, out, *rest):
    if row_width:
        rows, send_sem, recv_sem, own_sem, row_send, row_recv = rest
    else:
        send_sem, recv_sem, own_sem = rest
    outer, inner = wide_factors(wide)
    w, n = lax.axis_index("wide"), lax.axis_index("narrow")
    core = lax.rem(w, 2)
    y = lax.rem(w // 2, inner)
    z = w // (2 * inner)

    def wide_at(zz, yy, cc):
        return (zz * inner + yy) * 2 + cc

    def slot(zz, yy, cc, nn):
        return wide_at(zz, yy, cc) * narrow + nn

    xs = [lax.rem(n + i, narrow) for i in range(1, narrow)]
    zs = [lax.rem(z + i, outer) for i in range(1, outer)]
    ys = [lax.rem(y + i, inner) for i in range(1, inner)]
    to_x = [(w, nn) for nn in xs]
    to_z = [(wide_at(zz, y, core), n) for zz in zs]
    to_y = [(wide_at(z, yy, core), n) for yy in ys]
    to_core = [(wide_at(z, y, 1 - core), n)]
    peers = to_x + to_z + to_y + to_core

    barrier = pltpu.get_barrier_semaphore()
    for peer in peers:
        pl.semaphore_signal(barrier, inc=1, device_id=peer, device_id_type=MESH)
    pl.semaphore_wait(barrier, len(peers))

    def piece(nn):
        if split:
            return src.at[:, pl.ds(pl.multiple_of(nn * split, split), split)]
        return src

    started = []

    def send(ref, index, target):
        copy = pltpu.make_async_remote_copy(
            src_ref=ref,
            dst_ref=out.at[index],
            send_sem=send_sem.at[len(started)],
            recv_sem=recv_sem.at[index],
            device_id=target,
            device_id_type=MESH,
        )
        copy.start()
        started.append(copy)

    def arrived(index):
        pltpu.make_async_remote_copy(
            src_ref=out.at[index],
            dst_ref=out.at[index],
            send_sem=send_sem.at[0],
            recv_sem=recv_sem.at[index],
            device_id=to_core[0],
            device_id_type=MESH,
        ).wait_recv()

    if row_width:
        holder = w // (wide // narrow)
        first = pl.multiple_of(lax.rem(w, wide // narrow) * row_step, 128)
        group = 2 * narrow

    def row_copy(index, target, start, sem):
        return pltpu.make_async_remote_copy(
            src_ref=out.at[pl.ds(start, group), :, pl.ds(first, row_width)],
            dst_ref=rows.at[pl.ds(start, group)],
            send_sem=row_send.at[sem],
            recv_sem=row_recv.at[index],
            device_id=target,
            device_id_type=MESH,
        )

    chips = [(zz, yy) for yy in [y] + ys for zz in [z] + zs]

    def finish(number):
        zz, yy = chips[number]
        for nn in [n] + xs:
            arrived(slot(zz, yy, 1 - core, nn))
        if row_width:
            @pl.when(n == holder)
            def _():
                for k, target in enumerate(to_x):
                    row_copy(number, target, slot(zz, yy, 0, 0), number * len(to_x) + k).start()

    mine = slot(z, y, core, n)
    for target in to_x:
        send(piece(target[1]), mine, target)
    for target in to_z + to_y + to_core:
        send(piece(n), mine, target)
    own = pltpu.make_async_copy(piece(n), out.at[mine], own_sem)
    own.start()
    for nn in xs:
        index = slot(z, y, core, nn)
        arrived(index)
        for target in to_z + to_y + to_core:
            send(out.at[index], index, target)
    for zz in zs:
        for nn in [n] + xs:
            index = slot(zz, y, core, nn)
            arrived(index)
            for target in to_y + to_core:
                send(out.at[index], index, target)
    own.wait()
    for number in range(outer):
        finish(number)
    for number, (zz, yy) in enumerate(chips[outer:], outer):
        for nn in [n] + xs:
            index = slot(zz, yy, core, nn)
            arrived(index)
            send(out.at[index], index, to_core[0])
        if number > outer:
            finish(number - 1)
    if len(chips) > outer:
        finish(len(chips) - 1)

    for copy in started:
        copy.wait_send()
    if row_width:
        @pl.when(n == holder)
        def _():
            rows[...] = out[:, :, pl.ds(first, row_width)]
            for number, (zz, yy) in enumerate(chips):
                for k, target in enumerate(to_x):
                    row_copy(number, target, slot(zz, yy, 0, 0), number * len(to_x) + k).wait_send()

        @pl.when(n != holder)
        def _():
            for number, (zz, yy) in enumerate(chips):
                row_copy(number, to_x[0], slot(zz, yy, 0, 0), 0).wait_recv()


def gather(src, wide, narrow, split, row_width, row_step, collective_id):
    outer, inner = wide_factors(wide)
    devices = wide * narrow
    n_x, n_z, n_y = narrow - 1, outer - 1, inner - 1
    sends = n_x + n_z + n_y + 1
    sends += n_x * (n_z + n_y + 1) + n_z * narrow * (n_y + 1) + n_y * outer * narrow
    block = (src.shape[0], split or src.shape[1])
    out_shape = [jax.ShapeDtypeStruct((devices,) + block, src.dtype)]
    scratch = [
        pltpu.SemaphoreType.DMA((sends,)),
        pltpu.SemaphoreType.DMA((devices,)),
        pltpu.SemaphoreType.DMA,
    ]
    if row_width:
        out_shape.append(jax.ShapeDtypeStruct((devices, src.shape[0], row_width), src.dtype))
        scratch.append(pltpu.SemaphoreType.DMA((outer * inner * n_x,)))
        scratch.append(pltpu.SemaphoreType.DMA((outer * inner,)))
    return pl.pallas_call(
        functools.partial(gather_kernel, wide, narrow, split, row_width, row_step),
        out_shape=out_shape,
        in_specs=[pl.BlockSpec(memory_space=pl.ANY)],
        out_specs=[pl.BlockSpec(memory_space=VMEM if row_width else pl.ANY)] * len(out_shape),
        scratch_shapes=scratch,
        compiler_params=pltpu.CompilerParams(
            collective_id=collective_id, has_side_effects=True, vmem_limit_bytes=(48 if row_width else 63) << 20
        ),
    )(src)


@functools.lru_cache(None)
def tables(num_waves, num_val):
    fold = np.arange(GRID)
    fold = np.where(fold < GRID // 2, fold, fold - GRID)
    squares = fold**2
    lengths = (squares[:, None, None] + squares[None, :, None] + squares[None, None, :]).reshape(-1)
    limit = int(np.sort(lengths)[num_waves - 1])
    reach = math.isqrt(limit)
    assert reach < GRID // 2
    half = [
        (ky, kz)
        for ky in range(-reach, reach + 1)
        for kz in range(0, reach + 1)
        if ky * ky + kz * kz <= limit and (kz > 0 or ky >= 0)
    ]
    count = -(-len(half) // 128) * 128
    kys = np.array([k for k, _ in half])
    kzs = np.array([k for _, k in half])
    points = np.arange(GRID)
    turn = 2.0 * np.pi / GRID
    phase = (points[:, None, None] * kys + points[None, :, None] * kzs) % GRID
    phase = phase.reshape(GRID * GRID, len(half)) * turn
    plane = np.zeros((GRID * GRID, 2 * count))
    plane[:, : len(half)] = np.cos(phase)
    plane[:, count : count + len(half)] = -np.sin(phase)
    codes = np.full((count, 2), -1, np.int32)
    codes[: len(half), 0] = (kys % GRID) * GRID + kzs % GRID
    codes[: len(half), 1] = (-kys % GRID) * GRID + -kzs % GRID
    kxs = np.arange(-reach, reach + 1)
    line = (kxs[:, None] * points[None, :] % GRID) * turn
    eye = np.eye(num_val)
    norm = 1.0 / math.sqrt(GRID**3)
    cosine = np.kron(np.cos(line), eye) * norm
    sine = np.kron(np.sin(line), eye) * norm
    return plane, codes, np.stack([cosine, sine]), reach


MARGIN = 128


def window(tile):
    return tile // 2 + 2 * MARGIN


@functools.lru_cache(None)
def half_lists(num_waves, narrow, tiles):
    fold = np.arange(GRID)
    fold = np.where(fold < GRID // 2, fold, fold - GRID)
    kx, ky, kz = [k.reshape(-1) for k in np.meshgrid(fold, fold, fold, indexing="ij")]
    lengths = kx * kx + ky * ky + kz * kz
    ordered = np.sort(lengths)[:num_waves]
    half = (kz > 0) | ((kz == 0) & ((ky > 0) | ((ky == 0) & (kx >= 0))))
    chosen = np.nonzero(half & (lengths <= ordered[-1]))[0]
    chosen = chosen[np.argsort(lengths[chosen], kind="stable")]
    sizes = lengths[chosen]
    part = num_waves // narrow
    slots = part // 2 + 2 * MARGIN
    lists = np.full((narrow, 1, slots), -1, np.int32)
    for n in range(narrow):
        begin = np.searchsorted(sizes, ordered[n * part])
        end = np.searchsorted(sizes, ordered[(n + 1) * part - 1], side="right")
        assert end - begin + MARGIN <= slots
        lists[n, 0, MARGIN : MARGIN + end - begin] = chosen[begin:end]
        for tile in tiles:
            for t in range(part // tile):
                g = n * part + t * tile
                low = np.searchsorted(sizes, ordered[g]) - begin + MARGIN
                high = np.searchsorted(sizes, ordered[g + tile - 1], side="right") - begin + MARGIN
                assert t * tile // 2 <= low and high <= t * tile // 2 + window(tile)
    return lists


def np_halves(table):
    table = np.asarray(table, np.float32)
    high = table.astype(jnp.bfloat16)
    return high, (table - high.astype(np.float32)).astype(jnp.bfloat16)


def split_bf16(x):
    high = x.astype(jnp.bfloat16)
    return high, (x - high.astype(jnp.float32)).astype(jnp.bfloat16)


def dot(a, b):
    return jnp.dot(a, b, preferred_element_type=jnp.float32)


def dot3(a, b_high, b_low):
    a_high, a_low = split_bf16(a)
    return dot(a_high, b_high) + (dot(a_low, b_high) + dot(a_high, b_low))


def dot3_left(a_high, a_low, b):
    b_high, b_low = split_bf16(b)
    return dot(a_high, b_high) + (dot(a_high, b_low) + dot(a_low, b_high))


def pair_kernel(reach, tile, *refs):
    sources, out, field, picked = refs[:8], refs[8], refs[9], refs[10]
    held, sems = refs[11:19], refs[19]
    copies = [pltpu.make_async_copy(a, b, sems.at[i]) for i, (a, b) in enumerate(zip(sources, held))]
    for copy in copies:
        copy.start()
    val, cond, plane_h, plane_l, line_h, line_l, codes, gmap = held
    xs, num_val, plane = val.shape
    count = codes.shape[0]
    kinds = 2 * reach + 1
    copies[0].wait()
    copies[1].wait()
    field[...] = (val[...] * cond[...]).reshape(xs * num_val, plane)
    copies[2].wait()
    copies[3].wait()
    step = dot3(field[...], plane_h[...], plane_l[...])
    real, imag = step[:, :count], step[:, count:]
    size = kinds * num_val
    for copy in copies[4:]:
        copy.wait()
    cos_h, sin_h, cos_l, sin_l = line_h[0], line_h[1], line_l[0], line_l[1]
    picked[:size, :] = dot3_left(cos_h, cos_l, real) + dot3_left(sin_h, sin_l, imag)
    picked[size:, :] = dot3_left(cos_h, cos_l, imag) - dot3_left(sin_h, sin_l, real)
    source = picked[...].astype(jnp.bfloat16)
    first, second = codes[:, 0:1], codes[:, 1:2]

    def body(t, carry):
        here = pl.ds(pl.multiple_of(t * tile, tile), tile)
        index = gmap[:, here]
        kx = index // (GRID * GRID)
        code = index % (GRID * GRID)
        ky, kz = code // GRID, code % GRID
        kx = jnp.where(kx < GRID // 2, kx, kx - GRID)
        direct = ((kz > 0) & (kz < GRID // 2)) | ((kz == 0) & (ky < GRID // 2))
        kx = jnp.where(direct, kx, -kx) + reach
        sign = jnp.where(direct, 1.0, -1.0).astype(jnp.float32)
        hit = (code == first) | (code == second)
        columns = dot(source, jnp.where(hit, 1.0, 0.0).astype(jnp.bfloat16))
        columns = columns.reshape(2, kinds, num_val, tile)
        real = jnp.zeros((num_val, tile), jnp.float32)
        imag = jnp.zeros((num_val, tile), jnp.float32)
        for k in range(kinds):
            keep = jnp.broadcast_to(kx == k, (num_val, tile))
            real = jnp.where(keep, columns[0, k], real)
            imag = jnp.where(keep, columns[1, k], imag)
        out[:, here] = jnp.concatenate([real, imag * sign], axis=0).astype(jnp.bfloat16)
        return carry

    lax.fori_loop(0, out.shape[1] // tile, body, 0)


def transform_pairs(val, cond, gmap, num_waves):
    xs, num_val, plane = val.shape
    waves = gmap.shape[1]
    table, codes, line, reach = tables(num_waves, num_val)
    plane_h, plane_l = np_halves(table)
    line_h, line_l = np_halves(line)
    count = codes.shape[0]
    operands = (val, cond, plane_h, plane_l, line_h, line_l, codes, gmap)
    held = [pltpu.VMEM(x.shape, x.dtype) for x in operands]
    return pl.pallas_call(
        functools.partial(pair_kernel, reach, 512 if waves % 512 == 0 else 256),
        out_shape=jax.ShapeDtypeStruct((2 * num_val, waves), jnp.bfloat16),
        in_specs=[pl.BlockSpec(memory_space=pl.ANY)] * 8,
        out_specs=pl.BlockSpec(memory_space=VMEM),
        scratch_shapes=[
            pltpu.VMEM((xs * num_val, plane), jnp.float32),
            pltpu.VMEM((2 * (2 * reach + 1) * num_val, count), jnp.float32),
        ]
        + held
        + [pltpu.SemaphoreType.DMA((8,))],
        compiler_params=pltpu.CompilerParams(vmem_limit_bytes=62 << 20),
    )(*[jnp.asarray(x) for x in operands])


def expand(held, listed, index, num_val):
    depth, slots = held.shape
    tile = index.shape[1]
    area = GRID * GRID
    lx, ly, lz = listed // area, listed // GRID % GRID, listed % GRID
    mirror = (GRID - lx) % GRID * area + (GRID - ly) % GRID * GRID + (GRID - lz) % GRID
    mirror = jnp.where(listed < 0, -1, mirror)

    def column(row):
        turned = jnp.broadcast_to(row, (128, slots)).T
        return jnp.concatenate([turned] * (tile // 128), axis=1)

    hit = (index == column(listed)) | (index == column(mirror))
    values = dot(held, jnp.where(hit, 1.0, 0.0).astype(jnp.bfloat16))
    kx, ky, kz = index // area, index // GRID % GRID, index % GRID
    low = GRID // 2
    direct = ((kz > 0) & (kz < low)) | (
        (kz == 0) & (((ky > 0) & (ky < low)) | ((ky == 0) & (kx < low)))
    )
    sign = jnp.where(direct, 1.0, -1.0).astype(jnp.float32)
    row = lax.broadcasted_iota(jnp.int32, (depth, tile), 0)
    return values * jnp.where(row // num_val % 2 == 1, sign, 1.0)


def chi_kernel(num_cond, num_val, scalars, gmap, lists, rows, columns, out, scaled):
    num, row_width, tile = out.shape
    depth = rows.shape[0]
    narrow, wide = lists.shape[0], gmap.shape[1] // row_width
    w, n = lax.axis_index("wide"), lax.axis_index("narrow")
    step = pl.program_id(0)

    @pl.when(step == 0)
    def _():
        lane = lax.broadcasted_iota(jnp.int32, (1, depth), 1)
        band, orbital = lane // (2 * num_val), lane % num_val

        def pick(first, count, where):
            def select(i, held):
                return jnp.where(where == i, scalars[first + i], held)

            return lax.fori_loop(0, count, select, jnp.zeros((1, depth), jnp.float32))

        gap = pick(0, num_cond, band) - pick(num_cond, num_val, orbital)
        norm = math.sqrt(num_cond * num_val)
        first = pl.multiple_of(lax.rem(w, wide // narrow) * (row_width // 2), 128)
        listed = lists[w // (wide // narrow), :, pl.ds(first, rows.shape[1])]
        index = gmap[:, pl.ds(pl.multiple_of(w * row_width, 128), row_width)]
        turned = expand(rows[...], listed, index, num_val).T
        for i in range(num):
            omega = scalars[num_cond + num_val + i]
            weight = -2.0 * gap / (gap * gap + omega * omega) / norm
            scaled[i] = (turned * weight).astype(jnp.bfloat16)

    first = pl.multiple_of(step * (tile // 2), 128)
    here = pl.ds(first, window(tile))
    part = gmap.shape[1] // narrow
    index = gmap[:, pl.ds(pl.multiple_of(n * part + step * tile, 128), tile)]
    panel = expand(columns[:, here], lists[n, :, here], index, num_val).astype(jnp.bfloat16)
    for i in range(num):
        out[i] = dot(scaled[i], panel)


def chi_of(eps_cond, eps_val, omega, gmap, lists, rows, columns, row_width, width):
    depth, row_slots = rows.shape
    num = omega.shape[0]
    tile = min(512, width)
    grant = 4 * depth * (row_slots + columns.shape[1]) + 8 * num * row_width * tile
    grant += (2 * num + 16) * row_width * depth + 16 * depth * tile + (8 << 20)
    scalars = jnp.concatenate([eps_cond, eps_val, omega])
    return pl.pallas_call(
        functools.partial(chi_kernel, eps_cond.shape[0], eps_val.shape[0]),
        grid=(width // tile,),
        out_shape=jax.ShapeDtypeStruct((num, row_width, width), jnp.float32),
        in_specs=[
            pl.BlockSpec(memory_space=SMEM),
            pl.BlockSpec(gmap.shape, lambda c: (0, 0)),
            pl.BlockSpec(lists.shape, lambda c: (0, 0, 0)),
            pl.BlockSpec(rows.shape, lambda c: (0, 0)),
            pl.BlockSpec(columns.shape, lambda c: (0, 0)),
        ],
        out_specs=pl.BlockSpec((num, row_width, tile), lambda c: (0, 0, c)),
        scratch_shapes=[pltpu.VMEM((num, row_width, depth), jnp.bfloat16)],
        compiler_params=pltpu.CompilerParams(vmem_limit_bytes=min(grant, 60 << 20)),
    )(scalars, gmap, jnp.asarray(lists), rows, columns)


def body(valence, conduction, eps_val, eps_cond, omega, gmap):
    wide, narrow = lax.axis_size("wide"), lax.axis_size("narrow")
    devices = wide * narrow
    num_val, chunk = valence.shape
    num_local = conduction.shape[0]
    assert num_local == 1
    plane = GRID * GRID
    waves = gmap.shape[0]
    [full] = gather(valence, wide, narrow, 0, 0, 0, 0)
    if chunk != plane:
        full = full.reshape(GRID, devices // GRID, num_val, chunk)
        full = jnp.transpose(full, (0, 2, 1, 3)).reshape(GRID, num_val, plane)
    row_width, width = waves // wide, waves // narrow
    lists = half_lists(waves, narrow, (row_width, min(512, width)))
    wanted = np.maximum(lists.reshape(1, -1), 0)
    local = transform_pairs(full, conduction.reshape(GRID, 1, plane), wanted, waves)
    slots, row_slots = lists.shape[2], window(row_width)
    columns, rows = gather(local, wide, narrow, slots, row_slots, row_width // 2, 1)
    depth = devices * 2 * num_val
    columns, rows = columns.reshape(depth, slots), rows.reshape(depth, row_slots)
    spot = gmap.reshape(1, waves)
    return chi_of(eps_cond, eps_val, omega, spot, lists, rows, columns, row_width, width)


def solution(mesh):
    placed = (P(None, ("wide", "narrow")), P(("wide", "narrow"), None), P(), P(), P(), P())
    return jax.shard_map(
        body, mesh=mesh, in_specs=placed, out_specs=P(None, "wide", "narrow"), check_vma=False
    )
```

profile of v0, /device:TPU:0, one launch (start us, length us, event | category | flops | bytes accessed | tf_op | source)
XLA Modules:
  0.0 82.9 jit_solution(16302438596669603269)
XLA Ops:
  0.0 0.8 pad_maximum_fusion.scalars
  0.8 18.9 %shard_map.127.refs_0_ = f32[32,8,1024]{2,1,0:T(8,128)} custom-call(f32[8,1024]{1,0:T(8,128)} %src.1), custom_call_target="tpu_custom_call" | custom-call | tf_op jit(solution)/shard_map/pallas_call | solution.py:176
  19.7 8.0 %shard_map.128.src = bf16[16,4608]{1,0:T(8,128)(2,1)} custom-call(f32[32,8,1024]{2,1,0:T(8,128)} %shard_map.127.refs_0_, f32[32,1,1024]{2,1,0:T(1,128)} %bitcast.7, bf16[1024,512]{1,0:T(8,128)(2,1)} %constant.14.clone.refs_2_, bf16[1024,512]{1,0:T(8,128)(2,1)} %constant.15.clone.refs_3_, bf16[2,200,256]{2,1,0:T(8,128)(2,1)} %constant.16.clone.refs_4_, ...), custom_call_target="tpu_custom_call" | custom-call | tf_op jit(solution)/shard_map/pallas_call | solution.py:345
  27.7 0.0 copy-start
  27.7 0.9 %copy-done = bf16[16,4608]{1,0:T(8,128)(2,1)S(1)} copy-done((bf16[16,4608]{1,0:T(8,128)(2,1)S(1)}, bf16[16,4608]{1,0:T(8,128)(2,1)}, u32[]{:S(2)}) %copy-start) | copy-done | bytes 147480
  28.6 28.4 %shard_map.129 = (bf16[32,16,2304]{2,1,0:T(8,128)(2,1)S(1)}, bf16[32,16,512]{2,1,0:T(8,128)(2,1)S(1)}) custom-call(bf16[16,4608]{1,0:T(8,128)(2,1)S(1)} %copy-done), custom_call_target="tpu_custom_call" | custom-call | tf_op jit(solution)/shard_map/pallas_call | solution.py:176
  57.0 0.0 copy-start.1
  57.0 0.7 copy-done.1
  57.8 0.0 copy-start.2
  57.8 0.7 copy-done.2
  58.5 24.4 %shard_map.130 = f32[6,512,4096]{2,1,0:T(8,128)} custom-call(f32[46]{0:T(128)S(1)} %pad_maximum_fusion.scalars, s32[1,8192]{1,0:T(1,128)S(1)} %bitcast.6, s32[2,1,2304]{2,1,0:T(1,128)S(1)} %copy-done.2, bf16[512,512]{1,0:T(8,128)(2,1)S(1)} %bitcast.5, bf16[512,2304]{1,0:T(8,128)(2,1)S(1)} %bitcast.4), custom_call_target="tpu_custom_call" | custom-call | tf_op jit(solution)/shard_map/pallas_call | solution.py:429
Async XLA Ops:
  27.7 0.9 %copy-start = (bf16[16,4608]{1,0:T(8,128)(2,1)S(1)}, bf16[16,4608]{1,0:T(8,128)(2,1)}, u32[]{:S(2)}) copy-start(bf16[16,4608]{1,0:T(8,128)(2,1)} %shard_map.128.src) | copy-start | bytes 442372
  57.0 0.8 copy-start.1
  57.8 0.7 copy-start.2
where the time goes:
time: 84.2 us; the launch traced here: 82.9 us
  Pallas kernels  79.7 us (95%)
  local copies, waits for them, and re-layouts  2.38 us (3%)
    pallas_call x2, Pallas kernels, gather(): pl.pallas_call(functools.partial(gather_kernel, wide, narrow, split, row_...  47.3 us
    pallas_call x1, Pallas kernels, chi_of(): pl.pallas_call(functools.partial(chi_kernel, eps_cond.shape[0], eps_val.s...  24.4 us
    pallas_call x1, Pallas kernels, transform_pairs(): pl.pallas_call(functools.partial(pair_kernel, reach, 512 if waves % 512 =...  8.01 us
    unnamed x6, local copies, waits for them, and re-layouts  2.38 us

commit v1 on v0

v1 whole, which is shorter than its diff:
```python
import functools
import math

import jax
import jax.numpy as jnp
import numpy as np
from jax import lax
from jax.experimental import pallas as pl
from jax.experimental.pallas import tpu as pltpu
from jax.sharding import PartitionSpec as P

GRID = 32
MESH = pl.DeviceIdType.MESH
VMEM = pltpu.MemorySpace.VMEM
HBM = pltpu.MemorySpace.HBM
SMEM = pltpu.MemorySpace.SMEM


def wide_factors(wide):
    chips = wide // 2
    inner = 2 ** (int(math.log2(chips)) // 2)
    return chips // inner, inner


@functools.lru_cache(None)
def tables(num_waves, num_val):
    fold = np.arange(GRID)
    fold = np.where(fold < GRID // 2, fold, fold - GRID)
    squares = fold**2
    lengths = (squares[:, None, None] + squares[None, :, None] + squares[None, None, :]).reshape(-1)
    limit = int(np.sort(lengths)[num_waves - 1])
    reach = math.isqrt(limit)
    assert reach < GRID // 2
    half = [
        (ky, kz)
        for ky in range(-reach, reach + 1)
        for kz in range(0, reach + 1)
        if ky * ky + kz * kz <= limit and (kz > 0 or ky >= 0)
    ]
    count = -(-len(half) // 128) * 128
    kys = np.array([k for k, _ in half])
    kzs = np.array([k for _, k in half])
    points = np.arange(GRID)
    turn = 2.0 * np.pi / GRID
    phase = (points[:, None, None] * kys + points[None, :, None] * kzs) % GRID
    phase = phase.reshape(GRID * GRID, len(half)) * turn
    plane = np.zeros((GRID * GRID, 2 * count))
    plane[:, : len(half)] = np.cos(phase)
    plane[:, count : count + len(half)] = -np.sin(phase)
    codes = np.full((count, 2), -1, np.int32)
    codes[: len(half), 0] = (kys % GRID) * GRID + kzs % GRID
    codes[: len(half), 1] = (-kys % GRID) * GRID + -kzs % GRID
    kxs = np.arange(-reach, reach + 1)
    line = (kxs[:, None] * points[None, :] % GRID) * turn
    eye = np.eye(num_val)
    norm = 1.0 / math.sqrt(GRID**3)
    cosine = np.kron(np.cos(line), eye) * norm
    sine = np.kron(np.sin(line), eye) * norm
    return plane, codes, np.stack([cosine, sine]), reach


def round_up(count, step):
    return -(-count // step) * step


@functools.lru_cache(None)
def half_lists(num_waves, narrow, tiles):
    fold = np.arange(GRID)
    fold = np.where(fold < GRID // 2, fold, fold - GRID)
    kx, ky, kz = [k.reshape(-1) for k in np.meshgrid(fold, fold, fold, indexing="ij")]
    lengths = kx * kx + ky * ky + kz * kz
    ordered = np.sort(lengths)[:num_waves]
    half = (kz > 0) | ((kz == 0) & ((ky > 0) | ((ky == 0) & (kx >= 0))))
    chosen = np.nonzero(half & (lengths <= ordered[-1]))[0]
    chosen = chosen[np.argsort(lengths[chosen], kind="stable")]
    sizes = lengths[chosen]
    part = num_waves // narrow
    ends = []
    for n in range(narrow):
        begin = np.searchsorted(sizes, ordered[n * part])
        ends.append((begin, np.searchsorted(sizes, ordered[(n + 1) * part - 1], side="right")))
    below, above = 0, {tile: 0 for tile in tiles}
    for n, (begin, _) in enumerate(ends):
        for tile in tiles:
            for t in range(part // tile):
                g = n * part + t * tile
                low = np.searchsorted(sizes, ordered[g]) - begin - t * tile // 2
                high = np.searchsorted(sizes, ordered[g + tile - 1], side="right") - begin - t * tile // 2
                below, above[tile] = max(below, -int(low)), max(above[tile], int(high))
    windows = {tile: round_up(below + above[tile], 128) for tile in tiles}
    slots = max((part // tile - 1) * tile // 2 + windows[tile] for tile in tiles)
    slots = max(slots, round_up(below + max(end - begin for begin, end in ends), 128))
    lists = np.full((narrow, 1, slots), -1, np.int32)
    for n, (begin, end) in enumerate(ends):
        lists[n, 0, below : below + end - begin] = chosen[begin:end]
    return lists, windows


def np_halves(table):
    table = np.asarray(table, np.float32)
    high = table.astype(jnp.bfloat16)
    return high, (table - high.astype(np.float32)).astype(jnp.bfloat16)


def split_bf16(x):
    high = x.astype(jnp.bfloat16)
    return high, (x - high.astype(jnp.float32)).astype(jnp.bfloat16)


def dot(a, b):
    return jnp.dot(a, b, preferred_element_type=jnp.float32)


def dot3(a, b_high, b_low):
    a_high, a_low = split_bf16(a)
    return dot(a_high, b_high) + (dot(a_low, b_high) + dot(a_high, b_low))


def dot3_left(a_high, a_low, b):
    b_high, b_low = split_bf16(b)
    return dot(a_high, b_high) + (dot(a_high, b_low) + dot(a_low, b_high))


def flip(i, mask, size):
    assert size & (size - 1) == 0
    out, bit = i, 1
    while bit < size:
        if mask & bit:
            out = out + bit * (1 - 2 * lax.rem(i // bit, 2))
        bit *= 2
    return out


class Place:
    def __init__(self, wide, narrow):
        self.outer, self.inner = wide_factors(wide)
        self.wide, self.narrow = wide, narrow
        self.w, self.n = lax.axis_index("wide"), lax.axis_index("narrow")
        self.core = lax.rem(self.w, 2)
        self.y = lax.rem(self.w // 2, self.inner)
        self.z = self.w // (2 * self.inner)
        self.sizes = dict(z=self.outer, y=self.inner, x=narrow)

    def wide_at(self, zz, yy, cc):
        return (zz * self.inner + yy) * 2 + cc

    def slot(self, zz, yy, cc, nn):
        return self.wide_at(zz, yy, cc) * self.narrow + nn

    def moved(self, masks):
        return (
            flip(self.z, masks.get("z", 0), self.outer),
            flip(self.y, masks.get("y", 0), self.inner),
            flip(self.n, masks.get("x", 0), self.narrow),
        )

    def device(self, masks):
        zz, yy, nn = self.moved(masks)
        return (self.wide_at(zz, yy, self.core), nn)

    def peers(self):
        found = []
        for dim, size in self.sizes.items():
            found += [self.device({dim: m}) for m in range(1, size)]
        other = self.wide_at(self.z, self.y, 1 - self.core)
        found += [(other, flip(self.n, m, self.narrow)) for m in range(self.narrow)]
        return found


def count_first(sizes, order):
    a, b, c = [sizes[dim] for dim in order]
    return (a - 1 + b - 1 + c - 1 + 1) + (a - 1) * (b - 1 + c - 1 + 1) + (b - 1) * a * (c - 1 + 1) + (c - 1) * a * b


ORDERS = (("z", "y", "x"), ("z", "x", "y"))


def first_gather(place, order, src, view, send_sem, recv_sem):
    sizes = [place.sizes[dim] for dim in order]
    partner = (place.wide_at(place.z, place.y, 1 - place.core), place.n)
    count = [0]

    def send(ref, index, target):
        pltpu.make_async_remote_copy(
            src_ref=ref,
            dst_ref=view(index),
            send_sem=send_sem.at[count[0]],
            recv_sem=recv_sem.at[index],
            device_id=target,
            device_id_type=MESH,
        ).start()
        count[0] += 1

    def arrived(index):
        pltpu.make_async_remote_copy(
            src_ref=view(index),
            dst_ref=view(index),
            send_sem=send_sem.at[0],
            recv_sem=recv_sem.at[index],
            device_id=partner,
            device_id_type=MESH,
        ).wait_recv()

    def index_of(masks):
        zz, yy, nn = place.moved(masks)
        return place.slot(zz, yy, place.core, nn)

    mine = index_of({})
    for dim, size in zip(order, sizes):
        for m in range(size - 1, 0, -1):
            send(src, mine, place.device({dim: m}))
    send(src, mine, partner)
    for level in range(3):
        lower = [{}]
        for dim, size in zip(order[:level], sizes[:level]):
            lower = [{**masks, dim: m} for masks in lower for m in range(size)]
        for m in range(1, sizes[level]):
            for masks in lower:
                index = index_of({**masks, order[level]: m})
                arrived(index)
                for dim, size in zip(order[level + 1 :], sizes[level + 1 :]):
                    for k in range(size - 1, 0, -1):
                        send(view(index), index, place.device({dim: k}))
                send(view(index), index, partner)
    assert count[0] == count_first(place.sizes, order)


def pairs_kernel(wide, narrow, reach, slots, row_window, row_step, *refs):
    src, sources = refs[0], refs[1:8]
    cols, rows = refs[8:10]
    val, held = refs[10], refs[11:18]
    stage, picked, pick_hot, pick_x, pick_sign, local = refs[18:24]
    first_send, first_recv, own_sem, load_sem, send_sem, recv_sem, row_recv = refs[24:31]
    cond, plane_h, plane_l, line_h, line_l, codes, wanted = held
    place = Place(wide, narrow)
    core, n, w, z, y = place.core, place.n, place.w, place.z, place.y
    outer, inner = place.outer, place.inner
    grid, num_val, plane = val.shape
    chunk = src.shape[1]
    per = plane // chunk
    count = codes.shape[0]
    kinds = 2 * reach + 1
    size = kinds * num_val

    copies = [pltpu.make_async_copy(a, b, load_sem.at[i]) for i, (a, b) in enumerate(zip(sources, held))]
    for i in (5, 6, 0, 1, 2, 3, 4):
        copies[i].start()

    peers = place.peers()
    barrier = pltpu.get_barrier_semaphore()
    for peer in peers:
        pl.semaphore_signal(barrier, inc=1, device_id=peer, device_id_type=MESH)
    pl.semaphore_wait(barrier, len(peers))

    def view(index):
        if per == 1:
            return val.at[index]
        return val.at[index // per, :, pl.ds(pl.multiple_of(lax.rem(index, per) * chunk, chunk), chunk)]

    mine = place.slot(z, y, core, n)
    own = pltpu.make_async_copy(src, view(mine), own_sem)
    own.start()

    def prepare():
        copies[5].wait()
        copies[6].wait()
        first, second = codes[:, 0:1], codes[:, 1:2]
        tile = 256 if pick_hot.shape[1] % 256 == 0 else 128

        def body(t, carry):
            here = pl.ds(pl.multiple_of(t * tile, tile), tile)
            index = wanted[:, here]
            kx = index // (GRID * GRID)
            code = index % (GRID * GRID)
            ky, kz = code // GRID, code % GRID
            kx = jnp.where(kx < GRID // 2, kx, kx - GRID)
            direct = ((kz > 0) & (kz < GRID // 2)) | ((kz == 0) & (ky < GRID // 2))
            pick_x[:, here] = jnp.where(direct, kx, -kx) + reach
            pick_sign[:, here] = jnp.where(direct, 1.0, -1.0).astype(jnp.float32)
            hit = (code == first) | (code == second)
            pick_hot[:, here] = jnp.where(hit, 1.0, 0.0).astype(jnp.bfloat16)
            return carry

        lax.fori_loop(0, pick_hot.shape[1] // tile, body, 0)

    for side in range(2):
        @pl.when(core == side)
        def _():
            first_gather(place, ORDERS[side], src, view, first_send, first_recv)

    own.wait()
    prepare()
    step = narrow // per

    def flat(cc):
        copies_of = [(2 * q + cc) * step for q in range(wide // 2)]
        field = [(val[pl.ds(p, step)] * cond[pl.ds(p, step)]).reshape(step * num_val, plane) for p in copies_of]
        result = dot3(jnp.concatenate(field, axis=0), plane_h[...], plane_l[...])
        for q, p in enumerate(copies_of):
            part = result[q * step * num_val : (q + 1) * step * num_val]
            stage[pl.ds(p, step)] = part.reshape(step, num_val, 2 * count)

    for i in range(3):
        copies[i].wait()
    flat(core)
    for zz in range(outer):
        for yy in range(inner):
            for nn in range(narrow):
                index = place.slot(zz, yy, 1 - core, nn)
                pltpu.make_async_copy(view(index), view(index), first_recv.at[index]).wait()
    flat(1 - core)
    copies[3].wait()
    copies[4].wait()
    whole = stage[...].reshape(grid * num_val, 2 * count)
    real, imag = whole[:, :count], whole[:, count:]
    cos_h, sin_h, cos_l, sin_l = line_h[0], line_h[1], line_l[0], line_l[1]
    picked[:size, :] = (dot3_left(cos_h, cos_l, real) + dot3_left(sin_h, sin_l, imag)).astype(jnp.bfloat16)
    picked[size:, :] = (dot3_left(cos_h, cos_l, imag) - dot3_left(sin_h, sin_l, real)).astype(jnp.bfloat16)

    def pick(half, store):
        base = pl.multiple_of(half * slots, 128)
        for begin in range(0, slots, 512):
            tile = min(512, slots - begin)
            here = pl.ds(pl.multiple_of(base + begin, 128), tile)
            columns = dot(picked[...], pick_hot[:, here]).reshape(2, kinds, num_val, tile)
            kx = jnp.broadcast_to(pick_x[:, here], (num_val, tile))
            sign = pick_sign[:, here]
            real = jnp.zeros((num_val, tile), jnp.float32)
            imag = jnp.zeros((num_val, tile), jnp.float32)
            for k in range(kinds):
                keep = kx == k
                real = jnp.where(keep, columns[0, k], real)
                imag = jnp.where(keep, columns[1, k], imag)
            store(begin, tile, jnp.concatenate([real, imag * sign], axis=0).astype(jnp.bfloat16))

    partner = (place.wide_at(z, y, 1 - core), n)
    pending = []

    def send(src_ref, dst_ref, target, sem, when=None):
        k = len(pending)
        pltpu.make_async_remote_copy(
            src_ref=src_ref,
            dst_ref=dst_ref,
            send_sem=send_sem.at[k],
            recv_sem=sem,
            device_id=target,
            device_id_type=MESH,
        ).start()
        pending.append((when, src_ref.shape))

    def forward(index, target, when=None):
        send(cols.at[index], cols.at[index], target, recv_sem.at[index], when)

    def arrived(index):
        pltpu.make_async_copy(cols.at[index], cols.at[index], recv_sem.at[index]).wait()

    holder = w // (wide // narrow)
    window_of = lambda ww: pl.multiple_of(lax.rem(ww, wide // narrow) * row_step, 128)
    others = [m for m in range(1, narrow)]

    def row_sends(zz, yy, when):
        start = place.slot(zz, yy, core, 0)
        group = (zz * inner + yy) * 2 + core

        @pl.when(n == holder)
        def _():
            for cc in (core, 1 - core):
                ww = place.wide_at(z, y, cc)
                for m in others:
                    send(
                        cols.at[pl.ds(start, narrow), :, pl.ds(window_of(ww), row_window)],
                        rows.at[pl.ds(start, narrow)],
                        (ww, flip(n, m, narrow)),
                        row_recv.at[group],
                        (when, "row"),
                    )

    for m in range(narrow - 1, 0, -1):
        half = flip(n, m, narrow)

        def store(begin, tile, value, m=m):
            local[m - 1, :, begin : begin + tile] = value

        pick(half, store)
        send(local.at[m - 1], cols.at[mine], (w, half), recv_sem.at[mine])

    def store_own(begin, tile, value):
        cols[mine, :, begin : begin + tile] = value

    pick(n, store_own)
    right, left = (place.wide_at(z + 1, y, core), n), (place.wide_at(z - 1, y, core), n)

    def spread(index, when, go_right, go_left):
        if go_right:
            @pl.when(z < outer - 1)
            def _():
                forward(index, right, (when, "right"))
        if go_left:
            @pl.when(z > 0)
            def _():
                forward(index, left, (when, "left"))
        for m in range(1, inner):
            forward(index, place.device({"y": m}), (when, None))
        forward(index, partner, (when, None))

    spread(mine, None, True, True)
    for m in others:
        index = place.slot(z, y, core, flip(n, m, narrow))
        arrived(index)
        spread(index, None, True, True)
    row_sends(z, y, None)

    def side_blocks(zz, when):
        for m in range(1, inner):
            yy = flip(y, m, inner)
            for k in range(narrow):
                index = place.slot(zz, yy, core, flip(n, k, narrow))
                arrived(index)
                forward(index, partner, (when, None))
            row_sends(zz, yy, when)

    def present(offset):
        return (z + offset >= 0) & (z + offset < outer)

    for s in range(1, outer):
        for offset in (-s, s):
            @pl.when(present(offset))
            def _():
                for k in range(narrow):
                    index = place.slot(z + offset, y, core, flip(n, k, narrow))
                    arrived(index)
                    spread(index, offset, offset < 0, offset > 0)
                row_sends(z + offset, y, offset)
        if s == 1:
            side_blocks(z, None)
        else:
            for offset in (1 - s, s - 1):
                @pl.when(present(offset))
                def _():
                    side_blocks(z + offset, offset)
    for offset in (1 - outer, outer - 1) if outer > 1 else ():
        @pl.when(present(offset))
        def _():
            side_blocks(z + offset, offset)
    if outer == 1:
        side_blocks(z, None)

    for zz in range(outer):
        for yy in range(inner):
            for nn in range(narrow):
                arrived(place.slot(zz, yy, 1 - core, nn))

    @pl.when(n == holder)
    def _():
        rows[...] = cols[:, :, pl.ds(window_of(w), row_window)]

    @pl.when(n != holder)
    def _():
        for group in range(wide):
            rows_of = rows.at[pl.ds(group * narrow, narrow)]
            pltpu.make_async_copy(rows_of, rows_of, row_recv.at[group]).wait()

    def drain(k, shape):
        ref = cols.at[0] if len(shape) == 2 else rows.at[pl.ds(0, narrow)]
        pltpu.make_async_copy(ref, ref, send_sem.at[k]).wait()

    waits = {}
    for k, (when, shape) in enumerate(pending):
        when = when if isinstance(when, tuple) else (when, None)
        waits.setdefault(when, []).append((k, shape))
    for (offset, kind), items in waits.items():
        test = None
        if offset is not None:
            test = present(offset)
        extra = {"right": z < outer - 1, "left": z > 0, "row": n == holder}.get(kind)
        if extra is not None:
            test = extra if test is None else test & extra

        def all_of(items=items):
            for k, shape in items:
                drain(k, shape)

        if test is None:
            all_of()
        else:
            pl.when(test)(all_of)

    for side, order in enumerate(ORDERS):
        @pl.when(core == side)
        def _():
            for k in range(count_first(place.sizes, order)):
                pltpu.make_async_copy(src, src, first_send.at[k]).wait()


def second_sends(outer, inner, narrow):
    spread = 2 + (inner - 1) + 1
    row = 2 * (narrow - 1)
    sides = (inner - 1) * (narrow + row)
    total = narrow - 1 + narrow * spread + row + sides
    return total + 2 * (outer - 1) * (narrow * (spread - 1) + row + sides)


def gather_pairs(val, cond, num_waves, lists, row_window, row_step, wide, narrow):
    num_val, chunk = val.shape
    table, codes, line, reach = tables(num_waves, num_val)
    plane_h, plane_l = np_halves(table)
    line_h, line_l = np_halves(line)
    slots = lists.shape[2]
    wanted = np.maximum(lists.reshape(1, -1), 0)
    outer, inner = wide_factors(wide)
    devices = wide * narrow
    count = codes.shape[0]
    plane = GRID * GRID
    kinds = 2 * reach + 1
    operands = (cond, plane_h, plane_l, line_h, line_l, codes, wanted)
    held = [pltpu.VMEM(x.shape, x.dtype) for x in operands]
    sizes = dict(z=outer, y=inner, x=narrow)
    sends = max(count_first(sizes, order) for order in ORDERS)
    depth = 2 * num_val
    return pl.pallas_call(
        functools.partial(pairs_kernel, wide, narrow, reach, slots, row_window, row_step),
        out_shape=[
            jax.ShapeDtypeStruct((devices, depth, slots), jnp.bfloat16),
            jax.ShapeDtypeStruct((devices, depth, row_window), jnp.bfloat16),
        ],
        in_specs=[pl.BlockSpec(memory_space=pl.ANY)] * 8,
        out_specs=[pl.BlockSpec(memory_space=VMEM)] * 2,
        scratch_shapes=[pltpu.VMEM((GRID, num_val, plane), jnp.float32)]
        + held
        + [
            pltpu.VMEM((GRID, num_val, 2 * count), jnp.float32),
            pltpu.VMEM((2 * kinds * num_val, count), jnp.bfloat16),
            pltpu.VMEM((count, narrow * slots), jnp.bfloat16),
            pltpu.VMEM((1, narrow * slots), jnp.int32),
            pltpu.VMEM((1, narrow * slots), jnp.float32),
            pltpu.VMEM((narrow - 1, depth, slots), jnp.bfloat16),
            pltpu.SemaphoreType.DMA((sends,)),
            pltpu.SemaphoreType.DMA((devices,)),
            pltpu.SemaphoreType.DMA,
            pltpu.SemaphoreType.DMA((7,)),
            pltpu.SemaphoreType.DMA((second_sends(outer, inner, narrow),)),
            pltpu.SemaphoreType.DMA((devices,)),
            pltpu.SemaphoreType.DMA((wide,)),
        ],
        compiler_params=pltpu.CompilerParams(
            collective_id=0, has_side_effects=True, vmem_limit_bytes=48 << 20
        ),
    )(val, *[jnp.asarray(x) for x in operands])


def expand(held, listed, index, num_val):
    depth, slots = held.shape
    tile = index.shape[1]
    area = GRID * GRID
    lx, ly, lz = listed // area, listed // GRID % GRID, listed % GRID
    mirror = (GRID - lx) % GRID * area + (GRID - ly) % GRID * GRID + (GRID - lz) % GRID
    mirror = jnp.where(listed < 0, -1, mirror)

    def column(row):
        turned = jnp.broadcast_to(row, (128, slots)).T
        return jnp.concatenate([turned] * (tile // 128), axis=1)

    hit = (index == column(listed)) | (index == column(mirror))
    values = dot(held, jnp.where(hit, 1.0, 0.0).astype(jnp.bfloat16))
    kx, ky, kz = index // area, index // GRID % GRID, index % GRID
    low = GRID // 2
    direct = ((kz > 0) & (kz < low)) | (
        (kz == 0) & (((ky > 0) & (ky < low)) | ((ky == 0) & (kx < low)))
    )
    sign = jnp.where(direct, 1.0, -1.0).astype(jnp.float32)
    row = lax.broadcasted_iota(jnp.int32, (depth, tile), 0)
    return values * jnp.where(row // num_val % 2 == 1, sign, 1.0)


def chi_kernel(num_cond, num_val, window, scalars, gmap, lists, rows, columns, out, scaled):
    num, row_width, tile = out.shape
    depth = rows.shape[0]
    narrow, wide = lists.shape[0], gmap.shape[1] // row_width
    w, n = lax.axis_index("wide"), lax.axis_index("narrow")
    step = pl.program_id(0)

    @pl.when(step == 0)
    def _():
        lane = lax.broadcasted_iota(jnp.int32, (1, depth), 1)
        band, orbital = lane // (2 * num_val), lane % num_val

        def pick(first, count, where):
            def select(i, held):
                return jnp.where(where == i, scalars[first + i], held)

            return lax.fori_loop(0, count, select, jnp.zeros((1, depth), jnp.float32))

        gap = pick(0, num_cond, band) - pick(num_cond, num_val, orbital)
        norm = math.sqrt(num_cond * num_val)
        first = pl.multiple_of(lax.rem(w, wide // narrow) * (row_width // 2), 128)
        listed = lists[w // (wide // narrow), :, pl.ds(first, rows.shape[1])]
        index = gmap[:, pl.ds(pl.multiple_of(w * row_width, 128), row_width)]
        turned = expand(rows[...], listed, index, num_val).T
        for i in range(num):
            omega = scalars[num_cond + num_val + i]
            weight = -2.0 * gap / (gap * gap + omega * omega) / norm
            scaled[i] = (turned * weight).astype(jnp.bfloat16)

    first = pl.multiple_of(step * (tile // 2), 128)
    here = pl.ds(first, window)
    part = gmap.shape[1] // narrow
    index = gmap[:, pl.ds(pl.multiple_of(n * part + step * tile, 128), tile)]
    panel = expand(columns[:, here], lists[n, :, here], index, num_val).astype(jnp.bfloat16)
    for i in range(num):
        out[i] = dot(scaled[i], panel)


def chi_of(eps_cond, eps_val, omega, gmap, lists, rows, columns, row_width, width, tile, window):
    depth, row_slots = rows.shape
    num = omega.shape[0]
    grant = 4 * depth * (row_slots + columns.shape[1]) + 8 * num * row_width * tile
    grant += (2 * num + 16) * row_width * depth + 16 * depth * tile + (8 << 20)
    scalars = jnp.concatenate([eps_cond, eps_val, omega])
    return pl.pallas_call(
        functools.partial(chi_kernel, eps_cond.shape[0], eps_val.shape[0], window),
        grid=(width // tile,),
        out_shape=jax.ShapeDtypeStruct((num, row_width, width), jnp.float32),
        in_specs=[
            pl.BlockSpec(memory_space=SMEM),
            pl.BlockSpec(gmap.shape, lambda c: (0, 0)),
            pl.BlockSpec(lists.shape, lambda c: (0, 0, 0)),
            pl.BlockSpec(rows.shape, lambda c: (0, 0)),
            pl.BlockSpec(columns.shape, lambda c: (0, 0)),
        ],
        out_specs=pl.BlockSpec((num, row_width, tile), lambda c: (0, 0, c)),
        scratch_shapes=[pltpu.VMEM((num, row_width, depth), jnp.bfloat16)],
        compiler_params=pltpu.CompilerParams(vmem_limit_bytes=min(grant, 60 << 20)),
    )(scalars, gmap, jnp.asarray(lists), rows, columns)


def body(valence, conduction, eps_val, eps_cond, omega, gmap):
    wide, narrow = lax.axis_size("wide"), lax.axis_size("narrow")
    devices = wide * narrow
    num_val = valence.shape[0]
    assert conduction.shape[0] == 1
    plane = GRID * GRID
    waves = gmap.shape[0]
    row_width, width = waves // wide, waves // narrow
    tile = min(512, width)
    lists, windows = half_lists(waves, narrow, (row_width, tile))
    band = conduction.reshape(GRID, 1, plane)
    columns, rows = gather_pairs(
        valence, band, waves, lists, windows[row_width], row_width // 2, wide, narrow
    )
    depth = devices * 2 * num_val
    columns, rows = columns.reshape(depth, -1), rows.reshape(depth, -1)
    spot = gmap.reshape(1, waves)
    return chi_of(
        eps_cond, eps_val, omega, spot, lists, rows, columns, row_width, width, tile, windows[tile]
    )


def solution(mesh):
    placed = (P(None, ("wide", "narrow")), P(("wide", "narrow"), None), P(), P(), P(), P())
    return jax.shard_map(
        body, mesh=mesh, in_specs=placed, out_specs=P(None, "wide", "narrow"), check_vma=False
    )
```

time: 84.2 us -> 77.2 us (0.917)
  Pallas kernels: 79.7 us -> 66.8 us
  local copies, waits for them, and re-layouts: 2.38 us -> 9.07 us
    pallas_call x3 -> x1, Pallas kernels: 55.3 us -> 42.3 us  [gather_pairs(): pl.pallas_call(functools.partial(pairs_kernel, wide, narrow, reach, slots...]
    unnamed x6 -> x20, local copies, waits for them, and re-layouts: 2.38 us -> 9.07 us
where the time goes in v1:
time: 77.2 us; the launch traced here: 76.6 us
  Pallas kernels  66.8 us (87%)
  local copies, waits for them, and re-layouts  9.07 us (12%)
    pallas_call x1, Pallas kernels, gather_pairs(): pl.pallas_call(functools.partial(pairs_kernel, wide, narrow, reach, slots...  42.3 us
    pallas_call x1, Pallas kernels, chi_of(): pl.pallas_call(functools.partial(chi_kernel, eps_cond.shape[0], eps_val.s...  24.4 us
    unnamed x20, local copies, waits for them, and re-layouts  9.07 us

profile of v1, /device:TPU:0, one launch (start us, length us, event | category | flops | bytes accessed | tf_op | source)
XLA Modules:
  0.0 76.6 jit_solution(13612876601665882305)
XLA Ops:
  0.0 0.8 pad_maximum_fusion.scalars
  0.8 0.0 copy-start
  0.8 1.2 %copy-done = bf16[1024,512]{1,0:T(8,128)(2,1)S(1)} copy-done((bf16[1024,512]{1,0:T(8,128)(2,1)S(1)}, bf16[1024,512]{1,0:T(8,128)(2,1)}, u32[]{:S(2)}) %copy-start) | copy-done | bytes 1048600
  2.0 0.0 copy-start.1
  2.0 1.2 %copy-done.1 = bf16[1024,512]{1,0:T(8,128)(2,1)S(1)} copy-done((bf16[1024,512]{1,0:T(8,128)(2,1)S(1)}, bf16[1024,512]{1,0:T(8,128)(2,1)}, u32[]{:S(2)}) %copy-start.1) | copy-done | bytes 1048600
  3.2 0.0 copy-start.2
  3.2 0.9 %copy-done.2 = bf16[2,200,256]{2,1,0:T(8,128)(2,1)S(1)} copy-done((bf16[2,200,256]{2,1,0:T(8,128)(2,1)S(1)}, bf16[2,200,256]{2,1,0:T(8,128)(2,1)}, u32[]{:S(2)}) %copy-start.2) | copy-done | bytes 204824
  4.1 0.0 copy-start.3
  4.1 0.9 %copy-done.3 = bf16[2,200,256]{2,1,0:T(8,128)(2,1)S(1)} copy-done((bf16[2,200,256]{2,1,0:T(8,128)(2,1)S(1)}, bf16[2,200,256]{2,1,0:T(8,128)(2,1)}, u32[]{:S(2)}) %copy-start.3) | copy-done | bytes 204824
  5.1 0.0 copy-start.4
  5.1 0.9 %copy-done.4 = f32[1,32768]{1,0:T(1,128)S(1)} copy-done((f32[1,32768]{1,0:T(1,128)S(1)}, f32[1,32768]{1,0:T(1,128)}, u32[]{:S(2)}) %copy-start.4) | copy-done | bytes 131096
  6.0 0.0 copy-start.5
  6.0 0.9 %copy-done.5 = s32[256,2]{1,0:T(8,128)S(1)} copy-done((s32[256,2]{1,0:T(8,128)S(1)}, s32[256,2]{1,0:T(8,128)}, u32[]{:S(2)}) %copy-start.5) | copy-done | bytes 2072
  6.9 0.0 copy-start.6
  6.9 0.8 copy-done.6
  7.6 0.0 copy-start.8
  7.6 0.7 copy-done.8
  8.4 42.3 %shard_map.127 = (bf16[32,16,2176]{2,1,0:T(8,128)(2,1)S(1)}, bf16[32,16,384]{2,1,0:T(8,128)(2,1)S(1)}) custom-call(f32[8,1024]{1,0:T(8,128)S(1)} %copy-done.6, f32[32,1,1024]{2,1,0:T(1,128)S(1)} %bitcast.6, bf16[1024,512]{1,0:T(8,128)(2,1)S(1)} %copy-done.1, bf16[1024,512]{1,0:T(8,128)(2,1)S(1)} %copy-done, bf16[2,200,256]{2,1,0:T(8,128)(2,1)S(1)} %copy-done.3, ...), custom_call_target="tpu_custom_call" | custom-call | tf_op jit(solution)/shard_map/pallas_call | solution.py:520
  50.7 0.0 copy-start.7
  50.7 0.7 copy-done.7
  51.5 0.0 copy-start.9
  51.5 0.7 copy-done.9
  52.2 24.4 %shard_map.128 = f32[6,512,4096]{2,1,0:T(8,128)} custom-call(f32[46]{0:T(128)S(1)} %pad_maximum_fusion.scalars, s32[1,8192]{1,0:T(1,128)S(1)} %bitcast.7, s32[2,1,2176]{2,1,0:T(1,128)S(1)} %copy-done.9, bf16[512,384]{1,0:T(8,128)(2,1)S(1)} %bitcast.5, bf16[512,2176]{1,0:T(8,128)(2,1)S(1)} %bitcast.4), custom_call_target="tpu_custom_call" | custom-call | tf_op jit(solution)/shard_map/pallas_call | solution.py:619
Async XLA Ops:
  0.8 1.2 %copy-start = (bf16[1024,512]{1,0:T(8,128)(2,1)S(1)}, bf16[1024,512]{1,0:T(8,128)(2,1)}, u32[]{:S(2)}) copy-start(bf16[1024,512]{1,0:T(8,128)(2,1)} %constant.15.clone.refs_3_) | copy-start | bytes 3145732
  2.0 1.2 %copy-start.1 = (bf16[1024,512]{1,0:T(8,128)(2,1)S(1)}, bf16[1024,512]{1,0:T(8,128)(2,1)}, u32[]{:S(2)}) copy-start(bf16[1024,512]{1,0:T(8,128)(2,1)} %constant.14.clone.refs_2_) | copy-start | bytes 3145732
  3.2 0.9 %copy-start.2 = (bf16[2,200,256]{2,1,0:T(8,128)(2,1)S(1)}, bf16[2,200,256]{2,1,0:T(8,128)(2,1)}, u32[]{:S(2)}) copy-start(bf16[2,200,256]{2,1,0:T(8,128)(2,1)} %constant.17.clone.refs_5_) | copy-start | bytes 614404
  4.1 0.9 %copy-start.3 = (bf16[2,200,256]{2,1,0:T(8,128)(2,1)S(1)}, bf16[2,200,256]{2,1,0:T(8,128)(2,1)}, u32[]{:S(2)}) copy-start(bf16[2,200,256]{2,1,0:T(8,128)(2,1)} %constant.16.clone.refs_4_) | copy-start | bytes 614404
  5.1 0.9 %copy-start.4 = (f32[1,32768]{1,0:T(1,128)S(1)}, f32[1,32768]{1,0:T(1,128)}, u32[]{:S(2)}) copy-start(f32[1,32768]{1,0:T(1,128)} %param.14) | copy-start | bytes 393220
  6.0 0.9 %copy-start.5 = (s32[256,2]{1,0:T(8,128)S(1)}, s32[256,2]{1,0:T(8,128)}, u32[]{:S(2)}) copy-start(s32[256,2]{1,0:T(8,128)} %constant.18.clone.refs_6_) | copy-start | bytes 6148
  6.9 0.8 copy-start.6
  7.6 0.7 copy-start.8
  50.7 0.8 copy-start.7
  51.5 0.7 copy-start.9

commit v2 on v1

--- a/solution.py
+++ b/solution.py
@@ -175,7 +175,7 @@
 ORDERS = (("z", "y", "x"), ("z", "x", "y"))
 
 
-def first_gather(place, order, src, view, send_sem, recv_sem):
+def first_gather(place, order, src, view, send_sem, recv_sem, idle):
     sizes = [place.sizes[dim] for dim in order]
     partner = (place.wide_at(place.z, place.y, 1 - place.core), place.n)
     count = [0]
@@ -210,6 +210,7 @@
         for m in range(size - 1, 0, -1):
             send(src, mine, place.device({dim: m}))
     send(src, mine, partner)
+    idle()
     for level in range(3):
         lower = [{}]
         for dim, size in zip(order[:level], sizes[:level]):
@@ -225,25 +226,29 @@
     assert count[0] == count_first(place.sizes, order)
 
 
-def pairs_kernel(wide, narrow, reach, slots, row_window, row_step, *refs):
-    src, sources = refs[0], refs[1:8]
-    cols, rows = refs[8:10]
-    val, held = refs[10], refs[11:18]
-    stage, picked, pick_hot, pick_x, pick_sign, local = refs[18:24]
-    first_send, first_recv, own_sem, load_sem, send_sem, recv_sem, row_recv = refs[24:31]
-    cond, plane_h, plane_l, line_h, line_l, codes, wanted = held
+def pairs_kernel(wide, narrow, reach, slots, window, row_window, row_step, *refs):
+    energies = refs[:3]
+    src, sources = refs[3], refs[4:12]
+    panel_out, scaled_out = refs[12:14]
+    val, held = refs[14], refs[15:23]
+    stage, picked, pick_hot, pick_x, pick_sign, local = refs[23:29]
+    cols, rows, hot, hot_sign, row_hot, row_sign, weights, panel, scaled = refs[29:38]
+    eps_cond, eps_val, omega = refs[38:41]
+    first_send, first_recv, own_sem, load_sem, send_sem, recv_sem, row_recv, out_sem = refs[41:49]
+    cond, plane_h, plane_l, line_h, line_l, codes, lists, gmap = held
     place = Place(wide, narrow)
     core, n, w, z, y = place.core, place.n, place.w, place.z, place.y
     outer, inner = place.outer, place.inner
     grid, num_val, plane = val.shape
+    devices = wide * narrow
     chunk = src.shape[1]
     per = plane // chunk
     count = codes.shape[0]
     kinds = 2 * reach + 1
     size = kinds * num_val
 
-    copies = [pltpu.make_async_copy(a, b, load_sem.at[i]) for i, (a, b) in enumerate(zip(sources, held))]
-    for i in (5, 6, 0, 1, 2, 3, 4):
+    copies = [pltpu.make_async_copy(a, b, load_sem.at[i]) for i, (a, b) in enumerate(zip([*sources, *energies], [*held, eps_cond, eps_val, omega]))]
+    for i in (5, 6, 0, 1, 2, 3, 4, 7, 8, 9, 10):
         copies[i].start()
 
     peers = place.peers()
@@ -269,7 +274,7 @@
 
         def body(t, carry):
             here = pl.ds(pl.multiple_of(t * tile, tile), tile)
-            index = wanted[:, here]
+            index = jnp.maximum(lists[:, here], 0)
             kx = index // (GRID * GRID)
             code = index % (GRID * GRID)
             ky, kz = code // GRID, code % GRID
@@ -286,10 +291,9 @@
     for side in range(2):
         @pl.when(core == side)
         def _():
-            first_gather(place, ORDERS[side], src, view, first_send, first_recv)
+            first_gather(place, ORDERS[side], src, view, first_send, first_recv, prepare)
 
     own.wait()
-    prepare()
     step = narrow // per
 
     def flat(cc):
@@ -375,6 +379,91 @@
                         (when, "row"),
                     )
 
+    block = devices // outer
+    block_rows = block * 2 * num_val
+    tile = hot.shape[2]
+
+    def prepare_hot():
+        for copy in copies[7:]:
+            copy.wait()
+        num_cond, num = eps_cond.shape[0], omega.shape[0]
+        depth = panel.shape[0]
+        lane = lax.broadcasted_iota(jnp.int32, (1, depth), 1)
+        band, orbital = lane // (2 * num_val), lane % num_val
+
+        def choose(ref, where):
+            def select(i, held):
+                return jnp.where(where == i, ref[i], held)
+
+            return lax.fori_loop(0, ref.shape[0], select, jnp.zeros((1, depth), jnp.float32))
+
+        gap = choose(eps_cond, band) - choose(eps_val, orbital)
+        norm = math.sqrt(num_cond * num_val)
+        for i in range(num):
+            weights[i : i + 1, :] = -2.0 * gap / (gap * gap + omega[i] * omega[i]) / norm
+
+        row_width = row_hot.shape[1]
+        first = pl.multiple_of(holder * slots + lax.rem(w, wide // narrow) * row_step, 128)
+        index = gmap[:, pl.ds(pl.multiple_of(w * row_width, 128), row_width)]
+        row_hot[...], row_sign[...] = expansion(lists[:, pl.ds(first, row_window)], index)
+
+        def body(t, carry):
+            first = pl.multiple_of(n * slots + t * (tile // 2), 128)
+            here = pl.ds(pl.multiple_of(t * tile, 128), tile)
+            index = gmap[:, pl.ds(pl.multiple_of(n * (tile * hot.shape[0]) + t * tile, 128), tile)]
+            hot[t], hot_sign[:, here] = expansion(lists[:, pl.ds(first, window)], index)
+            return carry
+
+        lax.fori_loop(0, hot.shape[0], body, 0)
+
+    def signed(values, sign):
+        row = lax.broadcasted_iota(jnp.int32, values.shape, 0)
+        return values * jnp.where(row // num_val % 2 == 1, sign, 1.0)
+
+    def expand_block(zz):
+        first = zz * block
+        base = pl.multiple_of(zz * block_rows, 16)
+        for yy in range(inner):
+            for nn in range(narrow):
+                arrived(place.slot(zz, yy, 1 - core, nn))
+
+        def body(t, carry):
+            source = cols[pl.ds(first, block), :, pl.ds(pl.multiple_of(t * (tile // 2), 128), window)]
+            here = pl.ds(pl.multiple_of(t * tile, 128), tile)
+            values = dot(source.reshape(block_rows, window), hot[t])
+            panel[pl.ds(base, block_rows), here] = signed(values, hot_sign[:, here]).astype(jnp.bfloat16)
+            return carry
+
+        lax.fori_loop(0, hot.shape[0], body, 0)
+        block_copies(zz)[0].start()
+
+    def block_copies(zz):
+        here = pl.ds(pl.multiple_of(zz * block_rows, 128), block_rows)
+        return (
+            pltpu.make_async_copy(panel.at[here], panel_out.at[here], out_sem.at[0, zz]),
+            pltpu.make_async_copy(scaled.at[:, :, here], scaled_out.at[:, :, here], out_sem.at[1, zz]),
+        )
+
+    def scale_block(zz):
+        first = zz * block
+        here = pl.ds(pl.multiple_of(zz * block_rows, 128), block_rows)
+
+        @pl.when(n == holder)
+        def _():
+            rows[pl.ds(first, block)] = cols[pl.ds(first, block), :, pl.ds(window_of(w), row_window)]
+
+        @pl.when(n != holder)
+        def _():
+            for group in range(block // narrow):
+                rows_of = rows.at[pl.ds(first + group * narrow, narrow)]
+                pltpu.make_async_copy(rows_of, rows_of, row_recv.at[zz * (block // narrow) + group]).wait()
+
+        values = dot(rows[pl.ds(first, block)].reshape(block_rows, row_window), row_hot[...])
+        turned = signed(values, row_sign[...]).T
+        for i in range(scaled.shape[0]):
+            scaled[i, :, here] = (turned * weights[i : i + 1, here]).astype(jnp.bfloat16)
+        block_copies(zz)[1].start()
+
     for m in range(narrow - 1, 0, -1):
         half = flip(n, m, narrow)
 
@@ -404,6 +493,7 @@
         forward(index, partner, (when, None))
 
     spread(mine, None, True, True)
+    prepare_hot()
     for m in others:
         index = place.slot(z, y, core, flip(n, m, narrow))
         arrived(index)
@@ -422,43 +512,34 @@
     def present(offset):
         return (z + offset >= 0) & (z + offset < outer)
 
-    for s in range(1, outer):
+    def each(s, work):
+        if s == 0:
+            work(z, None)
+            return
         for offset in (-s, s):
             @pl.when(present(offset))
             def _():
-                for k in range(narrow):
-                    index = place.slot(z + offset, y, core, flip(n, k, narrow))
-                    arrived(index)
-                    spread(index, offset, offset < 0, offset > 0)
-                row_sends(z + offset, y, offset)
-        if s == 1:
-            side_blocks(z, None)
-        else:
-            for offset in (1 - s, s - 1):
-                @pl.when(present(offset))
-                def _():
-                    side_blocks(z + offset, offset)
-    for offset in (1 - outer, outer - 1) if outer > 1 else ():
-        @pl.when(present(offset))
-        def _():
-            side_blocks(z + offset, offset)
-    if outer == 1:
-        side_blocks(z, None)
+                work(z + offset, offset)
+
+    def line_blocks(zz, offset):
+        for k in range(narrow):
+            index = place.slot(zz, y, core, flip(n, k, narrow))
+            arrived(index)
+            spread(index, offset, offset < 0, offset > 0)
+        row_sends(zz, y, offset)
+
+    for s in range(1, outer + 2):
+        if s < outer:
+            each(s, line_blocks)
+        if s - 1 < outer:
+            each(s - 1, side_blocks)
+        if s >= 2:
+            each(s - 2, lambda zz, offset: expand_block(zz))
+            each(s - 2, lambda zz, offset: scale_block(zz))
 
     for zz in range(outer):
-        for yy in range(inner):
-            for nn in range(narrow):
-                arrived(place.slot(zz, yy, 1 - core, nn))
-
-    @pl.when(n == holder)
-    def _():
-        rows[...] = cols[:, :, pl.ds(window_of(w), row_window)]
-
-    @pl.when(n != holder)
-    def _():
-        for group in range(wide):
-            rows_of = rows.at[pl.ds(group * narrow, narrow)]
-            pltpu.make_async_copy(rows_of, rows_of, row_recv.at[group]).wait()
+        for copy in block_copies(zz):
+            copy.wait()
 
     def drain(k, shape):
         ref = cols.at[0] if len(shape) == 2 else rows.at[pl.ds(0, narrow)]
@@ -500,31 +581,33 @@
     return total + 2 * (outer - 1) * (narrow * (spread - 1) + row + sides)
 
 
-def gather_pairs(val, cond, num_waves, lists, row_window, row_step, wide, narrow):
+def gather_pairs(val, cond, gmap, energies, lists, window, row_window, row_width, tile, wide, narrow):
     num_val, chunk = val.shape
-    table, codes, line, reach = tables(num_waves, num_val)
+    waves = gmap.shape[1]
+    table, codes, line, reach = tables(waves, num_val)
     plane_h, plane_l = np_halves(table)
     line_h, line_l = np_halves(line)
     slots = lists.shape[2]
-    wanted = np.maximum(lists.reshape(1, -1), 0)
     outer, inner = wide_factors(wide)
     devices = wide * narrow
     count = codes.shape[0]
     plane = GRID * GRID
     kinds = 2 * reach + 1
-    operands = (cond, plane_h, plane_l, line_h, line_l, codes, wanted)
+    operands = (cond, plane_h, plane_l, line_h, line_l, codes, lists.reshape(1, -1), gmap)
     held = [pltpu.VMEM(x.shape, x.dtype) for x in operands]
     sizes = dict(z=outer, y=inner, x=narrow)
     sends = max(count_first(sizes, order) for order in ORDERS)
     depth = 2 * num_val
+    width = waves // narrow
+    num = energies[2].shape[0]
     return pl.pallas_call(
-        functools.partial(pairs_kernel, wide, narrow, reach, slots, row_window, row_step),
+        functools.partial(pairs_kernel, wide, narrow, reach, slots, window, row_window, row_width // 2),
         out_shape=[
-            jax.ShapeDtypeStruct((devices, depth, slots), jnp.bfloat16),
-            jax.ShapeDtypeStruct((devices, depth, row_window), jnp.bfloat16),
+            jax.ShapeDtypeStruct((devices * depth, width), jnp.bfloat16),
+            jax.ShapeDtypeStruct((num, row_width, devices * depth), jnp.bfloat16),
         ],
-        in_specs=[pl.BlockSpec(memory_space=pl.ANY)] * 8,
-        out_specs=[pl.BlockSpec(memory_space=VMEM)] * 2,
+        in_specs=[pl.BlockSpec(memory_space=HBM)] * 12,
+        out_specs=[pl.BlockSpec(memory_space=HBM)] * 2,
         scratch_shapes=[pltpu.VMEM((GRID, num_val, plane), jnp.float32)]
         + held
         + [
@@ -534,23 +617,35 @@
             pltpu.VMEM((1, narrow * slots), jnp.int32),
             pltpu.VMEM((1, narrow * slots), jnp.float32),
             pltpu.VMEM((narrow - 1, depth, slots), jnp.bfloat16),
+            pltpu.VMEM((devices, depth, slots), jnp.bfloat16),
+            pltpu.VMEM((devices, depth, row_window), jnp.bfloat16),
+            pltpu.VMEM((width // tile, window, tile), jnp.bfloat16),
+            pltpu.VMEM((1, width), jnp.float32),
+            pltpu.VMEM((row_window, row_width), jnp.bfloat16),
+            pltpu.VMEM((1, row_width), jnp.float32),
+            pltpu.VMEM((num, devices * depth), jnp.float32),
+            pltpu.VMEM((devices * depth, width), jnp.bfloat16),
+            pltpu.VMEM((num, row_width, devices * depth), jnp.bfloat16),
+        ]
+        + [pltpu.SMEM(x.shape, x.dtype) for x in energies]
+        + [
             pltpu.SemaphoreType.DMA((sends,)),
             pltpu.SemaphoreType.DMA((devices,)),
             pltpu.SemaphoreType.DMA,
-            pltpu.SemaphoreType.DMA((7,)),
+            pltpu.SemaphoreType.DMA((11,)),
             pltpu.SemaphoreType.DMA((second_sends(outer, inner, narrow),)),
             pltpu.SemaphoreType.DMA((devices,)),
             pltpu.SemaphoreType.DMA((wide,)),
+            pltpu.SemaphoreType.DMA((2, outer)),
         ],
         compiler_params=pltpu.CompilerParams(
-            collective_id=0, has_side_effects=True, vmem_limit_bytes=48 << 20
+            collective_id=0, has_side_effects=True, vmem_limit_bytes=63 << 20
         ),
-    )(val, *[jnp.asarray(x) for x in operands])
-
-
-def expand(held, listed, index, num_val):
-    depth, slots = held.shape
-    tile = index.shape[1]
+    )(*energies, val, *[jnp.asarray(x) for x in operands])
+
+
+def expansion(listed, index):
+    slots, tile = listed.shape[1], index.shape[1]
     area = GRID * GRID
     lx, ly, lz = listed // area, listed // GRID % GRID, listed % GRID
     mirror = (GRID - lx) % GRID * area + (GRID - ly) % GRID * GRID + (GRID - lz) % GRID
@@ -561,98 +656,96 @@
         return jnp.concatenate([turned] * (tile // 128), axis=1)
 
     hit = (index == column(listed)) | (index == column(mirror))
-    values = dot(held, jnp.where(hit, 1.0, 0.0).astype(jnp.bfloat16))
     kx, ky, kz = index // area, index // GRID % GRID, index % GRID
     low = GRID // 2
     direct = ((kz > 0) & (kz < low)) | (
         (kz == 0) & (((ky > 0) & (ky < low)) | ((ky == 0) & (kx < low)))
     )
     sign = jnp.where(direct, 1.0, -1.0).astype(jnp.float32)
-    row = lax.broadcasted_iota(jnp.int32, (depth, tile), 0)
-    return values * jnp.where(row // num_val % 2 == 1, sign, 1.0)
-
-
-def chi_kernel(num_cond, num_val, window, scalars, gmap, lists, rows, columns, out, scaled):
-    num, row_width, tile = out.shape
-    depth = rows.shape[0]
-    narrow, wide = lists.shape[0], gmap.shape[1] // row_width
-    w, n = lax.axis_index("wide"), lax.axis_index("narrow")
-    step = pl.program_id(0)
-
-    @pl.when(step == 0)
-    def _():
-        lane = lax.broadcasted_iota(jnp.int32, (1, depth), 1)
-        band, orbital = lane // (2 * num_val), lane % num_val
-
-        def pick(first, count, where):
-            def select(i, held):
-                return jnp.where(where == i, scalars[first + i], held)
-
-            return lax.fori_loop(0, count, select, jnp.zeros((1, depth), jnp.float32))
-
-        gap = pick(0, num_cond, band) - pick(num_cond, num_val, orbital)
-        norm = math.sqrt(num_cond * num_val)
-        first = pl.multiple_of(lax.rem(w, wide // narrow) * (row_width // 2), 128)
-        listed = lists[w // (wide // narrow), :, pl.ds(first, rows.shape[1])]
-        index = gmap[:, pl.ds(pl.multiple_of(w * row_width, 128), row_width)]
-        turned = expand(rows[...], listed, index, num_val).T
+    return jnp.where(hit, 1.0, 0.0).astype(jnp.bfloat16), sign
+
+
+def chi_kernel(tile, scaled_src, panel_src, out, scaled, panel, held, scaled_sem, panel_sem, sems):
+    num, row_width, depth = scaled.shape
+    steps = panel.shape[0]
+
+    def load(t):
+        here = pl.ds(pl.multiple_of(t * tile, 128), tile)
+        return pltpu.make_async_copy(panel_src.at[:, here], panel.at[t], panel_sem.at[t])
+
+    def take(i):
+        return pltpu.make_async_copy(scaled_src.at[i], scaled.at[i], scaled_sem.at[i])
+
+    def copy(slot, i, t):
+        here = pl.ds(pl.multiple_of(t * tile, 128), tile)
+        return pltpu.make_async_copy(held.at[slot, i], out.at[i, :, here], sems.at[slot, i])
+
+    load(0).start()
+    for i in range(num):
+        take(i).start()
+    for t in range(1, steps):
+        load(t).start()
+    load(0).wait()
+    for i in range(num):
+        take(i).wait()
+        held[0, i] = dot(scaled[i], panel[0])
+        copy(0, i, 0).start()
+
+    def body(t, carry):
+        slot = lax.rem(t, 2)
+        load(t).wait()
+
+        @pl.when(t >= 2)
+        def _():
+            for i in range(num):
+                copy(slot, i, t - 2).wait()
+
         for i in range(num):
-            omega = scalars[num_cond + num_val + i]
-            weight = -2.0 * gap / (gap * gap + omega * omega) / norm
-            scaled[i] = (turned * weight).astype(jnp.bfloat16)
-
-    first = pl.multiple_of(step * (tile // 2), 128)
-    here = pl.ds(first, window)
-    part = gmap.shape[1] // narrow
-    index = gmap[:, pl.ds(pl.multiple_of(n * part + step * tile, 128), tile)]
-    panel = expand(columns[:, here], lists[n, :, here], index, num_val).astype(jnp.bfloat16)
-    for i in range(num):
-        out[i] = dot(scaled[i], panel)
-
-
-def chi_of(eps_cond, eps_val, omega, gmap, lists, rows, columns, row_width, width, tile, window):
-    depth, row_slots = rows.shape
-    num = omega.shape[0]
-    grant = 4 * depth * (row_slots + columns.shape[1]) + 8 * num * row_width * tile
-    grant += (2 * num + 16) * row_width * depth + 16 * depth * tile + (8 << 20)
-    scalars = jnp.concatenate([eps_cond, eps_val, omega])
+            held[slot, i] = dot(scaled[i], panel[t])
+        for i in range(num):
+            copy(slot, i, t).start()
+        return carry
+
+    lax.fori_loop(1, steps, body, 0)
+    for t in range(max(0, steps - 2), steps):
+        for i in range(num):
+            copy(t % 2, i, t).wait()
+
+
+def chi_of(scaled, panel, tile):
+    num, row_width, depth = scaled.shape
+    width = panel.shape[1]
     return pl.pallas_call(
-        functools.partial(chi_kernel, eps_cond.shape[0], eps_val.shape[0], window),
-        grid=(width // tile,),
+        functools.partial(chi_kernel, tile),
         out_shape=jax.ShapeDtypeStruct((num, row_width, width), jnp.float32),
-        in_specs=[
-            pl.BlockSpec(memory_space=SMEM),
-            pl.BlockSpec(gmap.shape, lambda c: (0, 0)),
-            pl.BlockSpec(lists.shape, lambda c: (0, 0, 0)),
-            pl.BlockSpec(rows.shape, lambda c: (0, 0)),
-            pl.BlockSpec(columns.shape, lambda c: (0, 0)),
+        in_specs=[pl.BlockSpec(memory_space=HBM)] * 2,
+        out_specs=pl.BlockSpec(memory_space=HBM),
+        scratch_shapes=[
+            pltpu.VMEM(scaled.shape, jnp.bfloat16),
+            pltpu.VMEM((width // tile, depth, tile), jnp.bfloat16),
+            pltpu.VMEM((2, num, row_width, tile), jnp.float32),
+            pltpu.SemaphoreType.DMA((num,)),
+            pltpu.SemaphoreType.DMA((width // tile,)),
+            pltpu.SemaphoreType.DMA((2, num)),
         ],
-        out_specs=pl.BlockSpec((num, row_width, tile), lambda c: (0, 0, c)),
-        scratch_shapes=[pltpu.VMEM((num, row_width, depth), jnp.bfloat16)],
-        compiler_params=pltpu.CompilerParams(vmem_limit_bytes=min(grant, 60 << 20)),
-    )(scalars, gmap, jnp.asarray(lists), rows, columns)
+        compiler_params=pltpu.CompilerParams(vmem_limit_bytes=63 << 20),
+    )(scaled, panel)
 
 
 def body(valence, conduction, eps_val, eps_cond, omega, gmap):
     wide, narrow = lax.axis_size("wide"), lax.axis_size("narrow")
-    devices = wide * narrow
-    num_val = valence.shape[0]
     assert conduction.shape[0] == 1
-    plane = GRID * GRID
     waves = gmap.shape[0]
     row_width, width = waves // wide, waves // narrow
     tile = min(512, width)
     lists, windows = half_lists(waves, narrow, (row_width, tile))
-    band = conduction.reshape(GRID, 1, plane)
-    columns, rows = gather_pairs(
-        valence, band, waves, lists, windows[row_width], row_width // 2, wide, narrow
+    band = conduction.reshape(GRID, 1, GRID * GRID)
+    energies = (eps_cond, eps_val, omega)
+    panel, scaled = gather_pairs(
+        valence, band, gmap.reshape(1, waves), energies, lists, windows[tile], windows[row_width],
+        row_width, tile, wide, narrow,
     )
-    depth = devices * 2 * num_val
-    columns, rows = columns.reshape(depth, -1), rows.reshape(depth, -1)
-    spot = gmap.reshape(1, waves)
-    return chi_of(
-        eps_cond, eps_val, omega, spot, lists, rows, columns, row_width, width, tile, windows[tile]
-    )
+    return chi_of(scaled, panel, tile)
 
 
 def solution(mesh):

time: 77.2 us -> 66.7 us (0.86)
  local copies, waits for them, and re-layouts: 9.07 us -> 0 us
    unnamed x20 -> x0, local copies, waits for them, and re-layouts: 9.07 us -> none
    pallas_call x1, Pallas kernels: 24.4 us -> 21.7 us  [chi_of(): pl.pallas_call(functools.partial(chi_kernel, tile), out_shape=jax.ShapeDt...]
    pallas_call x1, Pallas kernels: 42.3 us -> 44.9 us  [gather_pairs(): pl.pallas_call(functools.partial(pairs_kernel, wide, narrow, reach, slots...]
where the time goes in v2:
time: 66.7 us; the launch traced here: 66.6 us
  Pallas kernels  66.6 us (100%)
    pallas_call x1, Pallas kernels, gather_pairs(): pl.pallas_call(functools.partial(pairs_kernel, wide, narrow, reach, slots...  44.9 us
    pallas_call x1, Pallas kernels, chi_of(): pl.pallas_call(functools.partial(chi_kernel, tile), out_shape=jax.ShapeDt...  21.7 us

profile of v2, /device:TPU:0, one launch (start us, length us, event | category | flops | bytes accessed | tf_op | source)
XLA Modules:
  0.0 66.6 jit_solution(14352084075017952250)
XLA Ops:
  0.0 44.9 %shard_map.118 = (bf16[512,4096]{1,0:T(8,128)(2,1)}, bf16[6,512,512]{2,1,0:T(8,128)(2,1)}) custom-call(f32[32]{0:T(128)} %refs_0_.1, f32[8]{0:T(128)} %refs_1_.1, f32[6]{0:T(128)} %refs_2_.1, f32[8,1024]{1,0:T(8,128)} %refs_3_.1, f32[32,1,1024]{2,1,0:T(1,128)} %bitcast.2, bf16[1024,512]{1,0:T(8,128)(2,1)} %constant.12.clone.refs_5_, ...), custom_call_target="tpu_custom_call" | custom-call | tf_op jit(solution)/shard_map/pallas_call | solution.py:603
  44.9 21.7 %shard_map.119 = f32[6,512,4096]{2,1,0:T(8,128)} custom-call(bf16[6,512,512]{2,1,0:T(8,128)(2,1)} %get-tuple-element.7.scaled_src, bf16[512,4096]{1,0:T(8,128)(2,1)} %get-tuple-element.8.panel_src), custom_call_target="tpu_custom_call" | custom-call | tf_op jit(solution)/shard_map/pallas_call | solution.py:718

commit v3 on v2

--- a/solution.py
+++ b/solution.py
@@ -164,20 +164,21 @@
             found += [self.device({dim: m}) for m in range(1, size)]
         other = self.wide_at(self.z, self.y, 1 - self.core)
         found += [(other, flip(self.n, m, self.narrow)) for m in range(self.narrow)]
+        for m in range(1, self.narrow):
+            for dim in ("y", "z"):
+                found += [self.device({dim: k, "x": m}) for k in range(1, self.sizes[dim])]
         return found
 
 
-def count_first(sizes, order):
-    a, b, c = [sizes[dim] for dim in order]
-    return (a - 1 + b - 1 + c - 1 + 1) + (a - 1) * (b - 1 + c - 1 + 1) + (b - 1) * a * (c - 1 + 1) + (c - 1) * a * b
-
-
-ORDERS = (("z", "y", "x"), ("z", "x", "y"))
-
-
-def first_gather(place, order, src, view, send_sem, recv_sem, idle):
-    sizes = [place.sizes[dim] for dim in order]
+def count_first(outer, plane):
+    return (outer - 1 + plane) + (outer - 1) * plane + (plane - 1) * outer
+
+
+def first_gather(place, src, view, send_sem, recv_sem, idle):
+    outer, inner, narrow = place.outer, place.inner, place.narrow
     partner = (place.wide_at(place.z, place.y, 1 - place.core), place.n)
+    around = [{"y": a, "x": b} for a in range(inner) for b in range(narrow) if a or b]
+    around.sort(key=lambda masks: -(masks["y"] > 0) - (masks["x"] > 0))
     count = [0]
 
     def send(ref, index, target):
@@ -192,49 +193,42 @@
         count[0] += 1
 
     def arrived(index):
-        pltpu.make_async_remote_copy(
-            src_ref=view(index),
-            dst_ref=view(index),
-            send_sem=send_sem.at[0],
-            recv_sem=recv_sem.at[index],
-            device_id=partner,
-            device_id_type=MESH,
-        ).wait_recv()
+        pltpu.make_async_copy(view(index), view(index), recv_sem.at[index]).wait()
 
     def index_of(masks):
         zz, yy, nn = place.moved(masks)
         return place.slot(zz, yy, place.core, nn)
 
     mine = index_of({})
-    for dim, size in zip(order, sizes):
-        for m in range(size - 1, 0, -1):
-            send(src, mine, place.device({dim: m}))
+    for m in range(outer - 1, 0, -1):
+        send(src, mine, place.device({"z": m}))
+    for masks in around:
+        send(src, mine, place.device(masks))
     send(src, mine, partner)
     idle()
-    for level in range(3):
-        lower = [{}]
-        for dim, size in zip(order[:level], sizes[:level]):
-            lower = [{**masks, dim: m} for masks in lower for m in range(size)]
-        for m in range(1, sizes[level]):
-            for masks in lower:
-                index = index_of({**masks, order[level]: m})
-                arrived(index)
-                for dim, size in zip(order[level + 1 :], sizes[level + 1 :]):
-                    for k in range(size - 1, 0, -1):
-                        send(view(index), index, place.device({dim: k}))
-                send(view(index), index, partner)
-    assert count[0] == count_first(place.sizes, order)
+    for m in range(1, outer):
+        index = index_of({"z": m})
+        arrived(index)
+        for masks in around:
+            send(view(index), index, place.device(masks))
+        send(view(index), index, partner)
+    for m in range(outer):
+        for masks in around:
+            index = index_of({**masks, "z": m})
+            arrived(index)
+            send(view(index), index, partner)
+    assert count[0] == count_first(outer, inner * narrow)
 
 
 def pairs_kernel(wide, narrow, reach, slots, window, row_window, row_step, *refs):
     energies = refs[:3]
     src, sources = refs[3], refs[4:12]
-    panel_out, scaled_out = refs[12:14]
+    panel, scaled = refs[12:14]
     val, held = refs[14], refs[15:23]
     stage, picked, pick_hot, pick_x, pick_sign, local = refs[23:29]
-    cols, rows, hot, hot_sign, row_hot, row_sign, weights, panel, scaled = refs[29:38]
-    eps_cond, eps_val, omega = refs[38:41]
-    first_send, first_recv, own_sem, load_sem, send_sem, recv_sem, row_recv, out_sem = refs[41:49]
+    cols, rows, hot, hot_sign, row_hot, row_sign, weights = refs[29:36]
+    eps_cond, eps_val, omega = refs[36:39]
+    first_send, first_recv, own_sem, load_sem, send_sem, recv_sem, row_recv = refs[39:46]
     cond, plane_h, plane_l, line_h, line_l, codes, lists, gmap = held
     place = Place(wide, narrow)
     core, n, w, z, y = place.core, place.n, place.w, place.z, place.y
@@ -288,10 +282,7 @@
 
         lax.fori_loop(0, pick_hot.shape[1] // tile, body, 0)
 
-    for side in range(2):
-        @pl.when(core == side)
-        def _():
-            first_gather(place, ORDERS[side], src, view, first_send, first_recv, prepare)
+    first_gather(place, src, view, first_send, first_recv, prepare)
 
     own.wait()
     step = narrow // per
@@ -434,15 +425,7 @@
             panel[pl.ds(base, block_rows), here] = signed(values, hot_sign[:, here]).astype(jnp.bfloat16)
             return carry
 
-        lax.fori_loop(0, hot.shape[0], body, 0)
-        block_copies(zz)[0].start()
-
-    def block_copies(zz):
-        here = pl.ds(pl.multiple_of(zz * block_rows, 128), block_rows)
-        return (
-            pltpu.make_async_copy(panel.at[here], panel_out.at[here], out_sem.at[0, zz]),
-            pltpu.make_async_copy(scaled.at[:, :, here], scaled_out.at[:, :, here], out_sem.at[1, zz]),
-        )
+        lax.fori_loop(0, hot.shape[0], body, 0, unroll=4)
 
     def scale_block(zz):
         first = zz * block
@@ -462,7 +445,6 @@
         turned = signed(values, row_sign[...]).T
         for i in range(scaled.shape[0]):
             scaled[i, :, here] = (turned * weights[i : i + 1, here]).astype(jnp.bfloat16)
-        block_copies(zz)[1].start()
 
     for m in range(narrow - 1, 0, -1):
         half = flip(n, m, narrow)
@@ -471,7 +453,19 @@
             local[m - 1, :, begin : begin + tile] = value
 
         pick(half, store)
-        send(local.at[m - 1], cols.at[mine], (w, half), recv_sem.at[mine])
+        piece = local.at[m - 1]
+        send(piece, cols.at[mine], (w, half), recv_sem.at[mine])
+        for k in range(1, inner):
+            send(piece, cols.at[mine], place.device({"y": k, "x": m}), recv_sem.at[mine])
+
+        @pl.when(z < outer - 1)
+        def _():
+            send(piece, cols.at[mine], (place.wide_at(z + 1, y, core), half), recv_sem.at[mine], (None, "right"))
+
+        @pl.when(z > 0)
+        def _():
+            send(piece, cols.at[mine], (place.wide_at(z - 1, y, core), half), recv_sem.at[mine], (None, "left"))
+
 
     def store_own(begin, tile, value):
         cols[mine, :, begin : begin + tile] = value
@@ -497,7 +491,7 @@
     for m in others:
         index = place.slot(z, y, core, flip(n, m, narrow))
         arrived(index)
-        spread(index, None, True, True)
+        forward(index, partner)
     row_sends(z, y, None)
 
     def side_blocks(zz, when):
@@ -536,10 +530,6 @@
         if s >= 2:
             each(s - 2, lambda zz, offset: expand_block(zz))
             each(s - 2, lambda zz, offset: scale_block(zz))
-
-    for zz in range(outer):
-        for copy in block_copies(zz):
-            copy.wait()
 
     def drain(k, shape):
         ref = cols.at[0] if len(shape) == 2 else rows.at[pl.ds(0, narrow)]
@@ -566,18 +556,15 @@
         else:
             pl.when(test)(all_of)
 
-    for side, order in enumerate(ORDERS):
-        @pl.when(core == side)
-        def _():
-            for k in range(count_first(place.sizes, order)):
-                pltpu.make_async_copy(src, src, first_send.at[k]).wait()
+    for k in range(count_first(outer, inner * narrow)):
+        pltpu.make_async_copy(src, src, first_send.at[k]).wait()
 
 
 def second_sends(outer, inner, narrow):
     spread = 2 + (inner - 1) + 1
     row = 2 * (narrow - 1)
     sides = (inner - 1) * (narrow + row)
-    total = narrow - 1 + narrow * spread + row + sides
+    total = (narrow - 1) * (3 + inner) + spread + narrow - 1 + row + sides
     return total + 2 * (outer - 1) * (narrow * (spread - 1) + row + sides)
 
 
@@ -595,8 +582,7 @@
     kinds = 2 * reach + 1
     operands = (cond, plane_h, plane_l, line_h, line_l, codes, lists.reshape(1, -1), gmap)
     held = [pltpu.VMEM(x.shape, x.dtype) for x in operands]
-    sizes = dict(z=outer, y=inner, x=narrow)
-    sends = max(count_first(sizes, order) for order in ORDERS)
+    sends = count_first(outer, inner * narrow)
     depth = 2 * num_val
     width = waves // narrow
     num = energies[2].shape[0]
@@ -607,7 +593,7 @@
             jax.ShapeDtypeStruct((num, row_width, devices * depth), jnp.bfloat16),
         ],
         in_specs=[pl.BlockSpec(memory_space=HBM)] * 12,
-        out_specs=[pl.BlockSpec(memory_space=HBM)] * 2,
+        out_specs=[pl.BlockSpec(memory_space=VMEM)] * 2,
         scratch_shapes=[pltpu.VMEM((GRID, num_val, plane), jnp.float32)]
         + held
         + [
@@ -624,8 +610,6 @@
             pltpu.VMEM((row_window, row_width), jnp.bfloat16),
             pltpu.VMEM((1, row_width), jnp.float32),
             pltpu.VMEM((num, devices * depth), jnp.float32),
-            pltpu.VMEM((devices * depth, width), jnp.bfloat16),
-            pltpu.VMEM((num, row_width, devices * depth), jnp.bfloat16),
         ]
         + [pltpu.SMEM(x.shape, x.dtype) for x in energies]
         + [
@@ -636,12 +620,11 @@
             pltpu.SemaphoreType.DMA((second_sends(outer, inner, narrow),)),
             pltpu.SemaphoreType.DMA((devices,)),
             pltpu.SemaphoreType.DMA((wide,)),
-            pltpu.SemaphoreType.DMA((2, outer)),
         ],
         compiler_params=pltpu.CompilerParams(
-            collective_id=0, has_side_effects=True, vmem_limit_bytes=63 << 20
+            collective_id=0, has_side_effects=True, vmem_limit_bytes=24 << 20
         ),
-    )(*energies, val, *[jnp.asarray(x) for x in operands])
+    )(*[pltpu.with_memory_space_constraint(jnp.asarray(x), HBM) for x in (*energies, val, *operands)])
 
 
 def expansion(listed, index):
@@ -665,35 +648,19 @@
     return jnp.where(hit, 1.0, 0.0).astype(jnp.bfloat16), sign
 
 
-def chi_kernel(tile, scaled_src, panel_src, out, scaled, panel, held, scaled_sem, panel_sem, sems):
+def chi_kernel(tile, scaled, panel, out, held, sems):
     num, row_width, depth = scaled.shape
-    steps = panel.shape[0]
-
-    def load(t):
-        here = pl.ds(pl.multiple_of(t * tile, 128), tile)
-        return pltpu.make_async_copy(panel_src.at[:, here], panel.at[t], panel_sem.at[t])
-
-    def take(i):
-        return pltpu.make_async_copy(scaled_src.at[i], scaled.at[i], scaled_sem.at[i])
+    steps = panel.shape[1] // tile
 
     def copy(slot, i, t):
         here = pl.ds(pl.multiple_of(t * tile, 128), tile)
         return pltpu.make_async_copy(held.at[slot, i], out.at[i, :, here], sems.at[slot, i])
 
-    load(0).start()
-    for i in range(num):
-        take(i).start()
-    for t in range(1, steps):
-        load(t).start()
-    load(0).wait()
-    for i in range(num):
-        take(i).wait()
-        held[0, i] = dot(scaled[i], panel[0])
-        copy(0, i, 0).start()
+    def product(slot, i, t):
+        held[slot, i] = dot(scaled[i], panel[:, pl.ds(pl.multiple_of(t * tile, 128), tile)])
 
     def body(t, carry):
         slot = lax.rem(t, 2)
-        load(t).wait()
 
         @pl.when(t >= 2)
         def _():
@@ -701,13 +668,23 @@
                 copy(slot, i, t - 2).wait()
 
         for i in range(num):
-            held[slot, i] = dot(scaled[i], panel[t])
+            product(slot, i, t)
         for i in range(num):
             copy(slot, i, t).start()
         return carry
 
-    lax.fori_loop(1, steps, body, 0)
-    for t in range(max(0, steps - 2), steps):
+    lax.fori_loop(0, steps - 1, body, 0)
+    last = steps - 1
+    for i in range(num):
+        if last >= 2:
+            copy(last % 2, i, last - 2).wait()
+        product(last % 2, i, last)
+        if i % 2 == 1:
+            copy(last % 2, i - 1, last).start()
+            copy(last % 2, i, last).start()
+    if num % 2:
+        copy(last % 2, num - 1, last).start()
+    for t in range(max(0, last - 1), steps):
         for i in range(num):
             copy(t % 2, i, t).wait()
 
@@ -718,17 +695,13 @@
     return pl.pallas_call(
         functools.partial(chi_kernel, tile),
         out_shape=jax.ShapeDtypeStruct((num, row_width, width), jnp.float32),
-        in_specs=[pl.BlockSpec(memory_space=HBM)] * 2,
+        in_specs=[pl.BlockSpec(memory_space=VMEM)] * 2,
         out_specs=pl.BlockSpec(memory_space=HBM),
         scratch_shapes=[
-            pltpu.VMEM(scaled.shape, jnp.bfloat16),
-            pltpu.VMEM((width // tile, depth, tile), jnp.bfloat16),
             pltpu.VMEM((2, num, row_width, tile), jnp.float32),
-            pltpu.SemaphoreType.DMA((num,)),
-            pltpu.SemaphoreType.DMA((width // tile,)),
             pltpu.SemaphoreType.DMA((2, num)),
         ],
-        compiler_params=pltpu.CompilerParams(vmem_limit_bytes=63 << 20),
+        compiler_params=pltpu.CompilerParams(vmem_limit_bytes=20 << 20),
     )(scaled, panel)
 
 

time: 66.7 us -> 60.8 us (0.912)
  Pallas kernels: 66.6 us -> 60.6 us
    pallas_call x1, Pallas kernels: 44.9 us -> 41.1 us  [gather_pairs(): pl.pallas_call(functools.partial(pairs_kernel, wide, narrow, reach, slots...]
    pallas_call x1, Pallas kernels: 21.7 us -> 19.5 us  [chi_of(): pl.pallas_call(functools.partial(chi_kernel, tile), out_shape=jax.ShapeDt...]
where the time goes in v3:
time: 60.8 us; the launch traced here: 60.7 us
  Pallas kernels  60.6 us (100%)
    pallas_call x1, Pallas kernels, gather_pairs(): pl.pallas_call(functools.partial(pairs_kernel, wide, narrow, reach, slots...  41.1 us
    pallas_call x1, Pallas kernels, chi_of(): pl.pallas_call(functools.partial(chi_kernel, tile), out_shape=jax.ShapeDt...  19.5 us

profile of v3, /device:TPU:0, one launch (start us, length us, event | category | flops | bytes accessed | tf_op | source)
XLA Modules:
  0.0 60.7 jit_solution(17719703530760108943)
XLA Ops:
  0.0 41.1 %shard_map.118 = (bf16[512,4096]{1,0:T(8,128)(2,1)S(1)}, bf16[6,512,512]{2,1,0:T(8,128)(2,1)S(1)}) custom-call(f32[32]{0:T(128)} %refs_0_.1, f32[8]{0:T(128)} %refs_1_.1, f32[6]{0:T(128)} %refs_2_.1, f32[8,1024]{1,0:T(8,128)} %refs_3_.1, f32[32,1,1024]{2,1,0:T(1,128)} %bitcast.2, bf16[1024,512]{1,0:T(8,128)(2,1)} %constant.12.clone.refs_5_, ...), custom_call_target="tpu_custom_call" | custom-call | tf_op jit(solution)/shard_map/pallas_call | solution.py:589
  41.1 19.5 %shard_map.119 = f32[6,512,4096]{2,1,0:T(8,128)} custom-call(bf16[6,512,512]{2,1,0:T(8,128)(2,1)S(1)} %get-tuple-element.7.scaled, bf16[512,4096]{1,0:T(8,128)(2,1)S(1)} %get-tuple-element.8.panel), custom_call_target="tpu_custom_call" | custom-call | tf_op jit(solution)/shard_map/pallas_call | solution.py:695

commit v4 on v3

--- a/solution.py
+++ b/solution.py
@@ -165,7 +165,7 @@
         other = self.wide_at(self.z, self.y, 1 - self.core)
         found += [(other, flip(self.n, m, self.narrow)) for m in range(self.narrow)]
         for m in range(1, self.narrow):
-            for dim in ("y", "z"):
+            for dim in ("y",):
                 found += [self.device({dim: k, "x": m}) for k in range(1, self.sizes[dim])]
         return found
 
@@ -218,6 +218,11 @@
             arrived(index)
             send(view(index), index, partner)
     assert count[0] == count_first(outer, inner * narrow)
+
+
+def chunks_of(slots):
+    cut = slots // 1024 * 512
+    return [(0, cut), (cut, slots - cut)] if cut else [(0, slots)]
 
 
 def pairs_kernel(wide, narrow, reach, slots, window, row_window, row_step, *refs):
@@ -240,6 +245,7 @@
     count = codes.shape[0]
     kinds = 2 * reach + 1
     size = kinds * num_val
+    chunks = chunks_of(slots)
 
     copies = [pltpu.make_async_copy(a, b, load_sem.at[i]) for i, (a, b) in enumerate(zip([*sources, *energies], [*held, eps_cond, eps_val, omega]))]
     for i in (5, 6, 0, 1, 2, 3, 4, 7, 8, 9, 10):
@@ -312,7 +318,7 @@
     picked[:size, :] = (dot3_left(cos_h, cos_l, real) + dot3_left(sin_h, sin_l, imag)).astype(jnp.bfloat16)
     picked[size:, :] = (dot3_left(cos_h, cos_l, imag) - dot3_left(sin_h, sin_l, real)).astype(jnp.bfloat16)
 
-    def pick(half, store):
+    def pick(half, store, ready):
         base = pl.multiple_of(half * slots, 128)
         for begin in range(0, slots, 512):
             tile = min(512, slots - begin)
@@ -327,6 +333,9 @@
                 real = jnp.where(keep, columns[0, k], real)
                 imag = jnp.where(keep, columns[1, k], imag)
             store(begin, tile, jnp.concatenate([real, imag * sign], axis=0).astype(jnp.bfloat16))
+            for number, (start, length) in enumerate(chunks):
+                if begin + tile == start + length:
+                    ready(number)
 
     partner = (place.wide_at(z, y, 1 - core), n)
     pending = []
@@ -343,11 +352,16 @@
         ).start()
         pending.append((when, src_ref.shape))
 
-    def forward(index, target, when=None):
-        send(cols.at[index], cols.at[index], target, recv_sem.at[index], when)
-
-    def arrived(index):
-        pltpu.make_async_copy(cols.at[index], cols.at[index], recv_sem.at[index]).wait()
+    def part(ref, number):
+        return ref.at[:, pl.ds(*chunks[number])]
+
+    def forward(index, number, target, when=None):
+        ref = part(cols.at[index], number)
+        send(ref, ref, target, recv_sem.at[index, number], when)
+
+    def arrived(index, number):
+        ref = part(cols.at[index], number)
+        pltpu.make_async_copy(ref, ref, recv_sem.at[index, number]).wait()
 
     holder = w // (wide // narrow)
     window_of = lambda ww: pl.multiple_of(lax.rem(ww, wide // narrow) * row_step, 128)
@@ -416,7 +430,8 @@
         base = pl.multiple_of(zz * block_rows, 16)
         for yy in range(inner):
             for nn in range(narrow):
-                arrived(place.slot(zz, yy, 1 - core, nn))
+                for number in range(len(chunks)):
+                    arrived(place.slot(zz, yy, 1 - core, nn), number)
 
         def body(t, carry):
             source = cols[pl.ds(first, block), :, pl.ds(pl.multiple_of(t * (tile // 2), 128), window)]
@@ -452,46 +467,38 @@
         def store(begin, tile, value, m=m):
             local[m - 1, :, begin : begin + tile] = value
 
-        pick(half, store)
-        piece = local.at[m - 1]
-        send(piece, cols.at[mine], (w, half), recv_sem.at[mine])
-        for k in range(1, inner):
-            send(piece, cols.at[mine], place.device({"y": k, "x": m}), recv_sem.at[mine])
-
-        @pl.when(z < outer - 1)
-        def _():
-            send(piece, cols.at[mine], (place.wide_at(z + 1, y, core), half), recv_sem.at[mine], (None, "right"))
-
-        @pl.when(z > 0)
-        def _():
-            send(piece, cols.at[mine], (place.wide_at(z - 1, y, core), half), recv_sem.at[mine], (None, "left"))
-
+        def ready(number, m=m, half=half):
+            piece, there = part(local.at[m - 1], number), part(cols.at[mine], number)
+            sem = recv_sem.at[mine, number]
+            send(piece, there, (w, half), sem)
+
+        pick(half, store, ready)
 
     def store_own(begin, tile, value):
         cols[mine, :, begin : begin + tile] = value
 
-    pick(n, store_own)
     right, left = (place.wide_at(z + 1, y, core), n), (place.wide_at(z - 1, y, core), n)
 
-    def spread(index, when, go_right, go_left):
+    def spread(index, number, when, go_right, go_left):
         if go_right:
             @pl.when(z < outer - 1)
             def _():
-                forward(index, right, (when, "right"))
+                forward(index, number, right, (when, "right"))
         if go_left:
             @pl.when(z > 0)
             def _():
-                forward(index, left, (when, "left"))
+                forward(index, number, left, (when, "left"))
         for m in range(1, inner):
-            forward(index, place.device({"y": m}), (when, None))
-        forward(index, partner, (when, None))
-
-    spread(mine, None, True, True)
+            forward(index, number, place.device({"y": m}), (when, None))
+        forward(index, number, partner, (when, None))
+
+    pick(n, store_own, lambda number: spread(mine, number, None, True, True))
     prepare_hot()
     for m in others:
         index = place.slot(z, y, core, flip(n, m, narrow))
-        arrived(index)
-        forward(index, partner)
+        for number in range(len(chunks)):
+            arrived(index, number)
+            spread(index, number, None, True, True)
     row_sends(z, y, None)
 
     def side_blocks(zz, when):
@@ -499,8 +506,9 @@
             yy = flip(y, m, inner)
             for k in range(narrow):
                 index = place.slot(zz, yy, core, flip(n, k, narrow))
-                arrived(index)
-                forward(index, partner, (when, None))
+                for number in range(len(chunks)):
+                    arrived(index, number)
+                    forward(index, number, partner, (when, None))
             row_sends(zz, yy, when)
 
     def present(offset):
@@ -518,8 +526,9 @@
     def line_blocks(zz, offset):
         for k in range(narrow):
             index = place.slot(zz, y, core, flip(n, k, narrow))
-            arrived(index)
-            spread(index, offset, offset < 0, offset > 0)
+            for number in range(len(chunks)):
+                arrived(index, number)
+                spread(index, number, offset, offset < 0, offset > 0)
         row_sends(zz, y, offset)
 
     for s in range(1, outer + 2):
@@ -532,9 +541,10 @@
             each(s - 2, lambda zz, offset: scale_block(zz))
 
     def drain(k, shape):
-        ref = cols.at[0] if len(shape) == 2 else rows.at[pl.ds(0, narrow)]
+        ref = cols.at[0, :, pl.ds(0, shape[1])] if len(shape) == 2 else rows.at[pl.ds(0, narrow)]
         pltpu.make_async_copy(ref, ref, send_sem.at[k]).wait()
 
+    assert len(pending) == send_sem.shape[0]
     waits = {}
     for k, (when, shape) in enumerate(pending):
         when = when if isinstance(when, tuple) else (when, None)
@@ -560,12 +570,11 @@
         pltpu.make_async_copy(src, src, first_send.at[k]).wait()
 
 
-def second_sends(outer, inner, narrow):
-    spread = 2 + (inner - 1) + 1
-    row = 2 * (narrow - 1)
-    sides = (inner - 1) * (narrow + row)
-    total = (narrow - 1) * (3 + inner) + spread + narrow - 1 + row + sides
-    return total + 2 * (outer - 1) * (narrow * (spread - 1) + row + sides)
+def second_sends(outer, inner, narrow, chunks):
+    near = 2 * (outer - 1)
+    pieces = (narrow - 1) * 1 + narrow * (inner + 2) + 0 * inner
+    pieces += near * narrow * (inner + 1) + (near + 1) * (inner - 1) * narrow
+    return pieces * chunks + (near + 1) * inner * 2 * (narrow - 1)
 
 
 def gather_pairs(val, cond, gmap, energies, lists, window, row_window, row_width, tile, wide, narrow):
@@ -617,8 +626,8 @@
             pltpu.SemaphoreType.DMA((devices,)),
             pltpu.SemaphoreType.DMA,
             pltpu.SemaphoreType.DMA((11,)),
-            pltpu.SemaphoreType.DMA((second_sends(outer, inner, narrow),)),
-            pltpu.SemaphoreType.DMA((devices,)),
+            pltpu.SemaphoreType.DMA((second_sends(outer, inner, narrow, len(chunks_of(slots))),)),
+            pltpu.SemaphoreType.DMA((devices, len(chunks_of(slots)))),
             pltpu.SemaphoreType.DMA((wide,)),
         ],
         compiler_params=pltpu.CompilerParams(

time: 60.8 us -> 60.7 us (level)
  no operation moved by 1% of the time
where the time goes in v4:
time: 60.7 us; the launch traced here: 60.5 us
  Pallas kernels  60.5 us (100%)
    pallas_call x1, Pallas kernels, gather_pairs(): pl.pallas_call(functools.partial(pairs_kernel, wide, narrow, reach, slots...  41 us
    pallas_call x1, Pallas kernels, chi_of(): pl.pallas_call(functools.partial(chi_kernel, tile), out_shape=jax.ShapeDt...  19.5 us

profile of v4, /device:TPU:0, one launch (start us, length us, event | category | flops | bytes accessed | tf_op | source)
XLA Modules:
  0.0 60.5 jit_solution(1524141349067642863)
XLA Ops:
  0.0 41.0 %shard_map.118 = (bf16[512,4096]{1,0:T(8,128)(2,1)S(1)}, bf16[6,512,512]{2,1,0:T(8,128)(2,1)S(1)}) custom-call(f32[32]{0:T(128)} %refs_0_.1, f32[8]{0:T(128)} %refs_1_.1, f32[6]{0:T(128)} %refs_2_.1, f32[8,1024]{1,0:T(8,128)} %refs_3_.1, f32[32,1,1024]{2,1,0:T(1,128)} %bitcast.2, bf16[1024,512]{1,0:T(8,128)(2,1)} %constant.12.clone.refs_5_, ...), custom_call_target="tpu_custom_call" | custom-call | tf_op jit(solution)/shard_map/pallas_call | solution.py:598
  41.0 19.5 %shard_map.119 = f32[6,512,4096]{2,1,0:T(8,128)} custom-call(bf16[6,512,512]{2,1,0:T(8,128)(2,1)S(1)} %get-tuple-element.7.scaled, bf16[512,4096]{1,0:T(8,128)(2,1)S(1)} %get-tuple-element.8.panel), custom_call_target="tpu_custom_call" | custom-call | tf_op jit(solution)/shard_map/pallas_call | solution.py:704
